TPU v7x, 256 devices: a whole 4x4x8 slice. The times are simulated.
256 devices in a mesh: ka: 32 (over x_hi, z, core), band: 8 (over x_lo, y).
Axes of the slice: x: 4 (x_hi: 2, x_lo: 2; x = x_hi * 2 + x_lo), y: 4, z: 8, core: 2. Of those that a mesh axis runs over, the one named last changes fastest.
Arguments:
- valence_orbitals: bfloat16 [32, 32, 64, 64, 128], P('ka', None, None, 'band'), may hold values from -6 to 6
- conduction_orbitals: bfloat16 [32, 1, 64, 64, 128], P(None, None, 'ka', 'band'), may hold values from -6 to 6
- valence_energy: float32 [32, 32], P('ka'), may hold values from -1.5 to -0.1
- conduction_energy: float32 [32, 1], replicated, may hold values from 0.1 to 1.5
- valence_select: int32 [32, 16], P('ka'), may hold values from 0 to 31, as said below
- shifted_index: int32 [32], replicated, may hold values from 0 to 31, each once
- wave_vectors: int32 [3, 2048], replicated, may hold values from -16 to 15
- frequency: float32 [1], replicated, may hold values from 0.3 to 1
Outputs:
- chi_zero: float32 [2, 2048, 2048], P(None, ('ka', 'band'))
Inputs may be any that keep to these rules, and one draw needn't show every extreme that they name: `valence_select`: each row holds 16 different band numbers. `shifted_index`: every k point is the partner of exactly one k point.
All inputs are finite; a program needn't handle non-finite values.
Results may differ from a plain program's by a relative error of at most 0.025.
Values may be sent and summed in bfloat16 or wider, within the bound.
No kernel may reach another device: no remote copies, remote signals or barrier semaphores. Data moves between devices by JAX's collectives and lax.ppermute only.
A program may use at most 256 MiB of HBM per device.

v0:
```python
import math

import jax
import jax.numpy as jnp
from jax import lax
from jax.sharding import PartitionSpec as P


def depth_matrix(grid_size):
    positions = jnp.arange(grid_size, dtype=jnp.int32)
    phase_index = positions[:, None] * positions[None, :] % grid_size
    angle_value = phase_index.astype(jnp.float32) * (2.0 * math.pi / grid_size)
    cosine = jnp.cos(angle_value)
    sine_part = jnp.sin(angle_value)
    upper_half = jnp.concatenate([cosine, -sine_part], axis=1)
    lower_half = jnp.concatenate([sine_part, cosine], axis=1)
    return jnp.concatenate([upper_half, lower_half], axis=0).astype(jnp.bfloat16)


def column_matrix(grid_size):
    positions = jnp.arange(grid_size, dtype=jnp.int32)
    phase_index = positions[:, None] * positions[None, :] % grid_size
    angle_value = phase_index.astype(jnp.float32) * (2.0 * math.pi / grid_size)
    return jnp.concatenate([jnp.cos(angle_value), jnp.sin(angle_value)], axis=0).astype(
        jnp.bfloat16
    )


def shards(
    valence_orbitals,
    conduction_orbitals,
    valence_energy,
    conduction_energy,
    valence_select,
    shifted_index,
    wave_vectors,
    frequency,
):
    grid_size = valence_orbitals.shape[2]
    slab_width = valence_orbitals.shape[3]
    kpoint_count = lax.axis_size("ka")
    band_count = lax.axis_size("band")
    kpoint_rank = lax.axis_index("ka")
    band_rank = lax.axis_index("band")
    vector_count = wave_vectors.shape[1]
    block_rows = vector_count // (kpoint_count * band_count)
    share_size = vector_count // band_count
    permuted = (
        wave_vectors.reshape(3, kpoint_count, band_count, block_rows)
        .transpose(0, 2, 1, 3)
        .reshape(3, vector_count)
    )
    wrapped = jnp.mod(permuted, grid_size)
    twice = 2 * grid_size
    first_index = wrapped[1] * twice + wrapped[2]
    second_index = (grid_size + wrapped[1]) * twice + grid_size + wrapped[2]
    third_index = wrapped[1] * twice + grid_size + wrapped[2]
    fourth_index = (grid_size + wrapped[1]) * twice + wrapped[2]
    plane_coord = band_rank * slab_width + jnp.arange(slab_width, dtype=jnp.int32)
    plane_phase = wrapped[0][None, :] * plane_coord[:, None] % grid_size
    plane_angle = plane_phase.astype(jnp.float32) * (2.0 * math.pi / grid_size)
    norm_scale = float(grid_size) ** (-1.5)
    plane_cos = jnp.cos(plane_angle) * norm_scale
    plane_sin = jnp.sin(plane_angle) * norm_scale
    depth_table = depth_matrix(grid_size)
    column_table = column_matrix(grid_size)
    selected = jnp.take(valence_orbitals[0], valence_select[0], axis=0)
    selected_count = selected.shape[0]
    val_energies = jnp.take(valence_energy[0], valence_select[0])
    partner = shifted_index[kpoint_rank]
    cond_energies = lax.dynamic_index_in_dim(conduction_energy, partner, 0, keepdims=False)
    energy_gap = val_energies[None, :] - cond_energies[:, None]
    weight = (
        2.0
        * energy_gap
        / (energy_gap * energy_gap + frequency[0] * frequency[0])
        / (kpoint_count * selected_count)
    )

    def item_terms(columns):
        cond_real = columns[..., :grid_size].astype(jnp.float32)
        cond_imag = columns[..., grid_size:].astype(jnp.float32)
        val_real = selected[..., :grid_size].astype(jnp.float32)
        val_imag = selected[..., grid_size:].astype(jnp.float32)
        pair_values = jnp.concatenate(
            [
                val_real * cond_real[None] + val_imag * cond_imag[None],
                val_real * cond_imag[None] - val_imag * cond_real[None],
            ],
            axis=-1,
        ).astype(jnp.bfloat16)
        spectrum = jnp.dot(
            pair_values.reshape(-1, twice), depth_table, preferred_element_type=jnp.float32
        )
        spectrum = spectrum.astype(jnp.bfloat16).reshape(pair_values.shape)
        mixed_part = jnp.einsum(
            "ky,nyxc->nxkc", column_table, spectrum, preferred_element_type=jnp.float32
        )
        flat_view = mixed_part.reshape(selected_count, slab_width, twice * twice)
        real_cols = jnp.take(flat_view, first_index, axis=2) + jnp.take(
            flat_view, second_index, axis=2
        )
        imag_cols = jnp.take(flat_view, third_index, axis=2) - jnp.take(
            flat_view, fourth_index, axis=2
        )
        density_real = jnp.sum(plane_cos[None] * real_cols + plane_sin[None] * imag_cols, axis=1)
        density_imag = jnp.sum(plane_cos[None] * imag_cols - plane_sin[None] * real_cols, axis=1)
        return jnp.stack([density_real, density_imag])

    reordered = jnp.take(conduction_orbitals, shifted_index, axis=0)
    partial_value = lax.map(
        item_terms, lax.all_to_all(reordered, "ka", split_axis=0, concat_axis=2, tiled=True)[0]
    )
    summed = lax.psum(partial_value.astype(jnp.bfloat16), "band")
    own_share = lax.dynamic_slice_in_dim(summed, band_rank * share_size, share_size, 3)
    weighted = (weight[:, None, :, None] * own_share.astype(jnp.float32)).astype(jnp.bfloat16)
    contract_dims = (((0, 1, 2), (0, 1, 2)), ((), ()))
    swapped = jnp.stack([weighted[:, 1], -weighted[:, 0]], axis=1)
    real_rows = lax.dot_general(weighted, summed, contract_dims, preferred_element_type=jnp.float32)
    imag_rows = lax.dot_general(swapped, summed, contract_dims, preferred_element_type=jnp.float32)
    chi_block = lax.psum_scatter(
        jnp.stack([real_rows, imag_rows], axis=1).astype(jnp.bfloat16),
        "ka",
        scatter_dimension=0,
        tiled=True,
    ).astype(jnp.float32)
    chi_block = chi_block.reshape(block_rows, 2, band_count, kpoint_count, block_rows).transpose(
        0, 1, 3, 2, 4
    )
    chi_block = chi_block.reshape(block_rows, 2, vector_count)
    return chi_block.transpose(1, 0, 2)


def solution(mesh):
    in_specs = (
        P("ka", None, None, "band", None),
        P(None, None, "ka", "band", None),
        P("ka", None),
        P(),
        P("ka", None),
        P(),
        P(),
        P(),
    )
    out_specs = P(None, ("ka", "band"), None)
    return jax.shard_map(shards, mesh=mesh, in_specs=in_specs, out_specs=out_specs, check_vma=False)
```

profile of v0, /device:TPU:1, one launch (start us, length us, event | category | flops | bytes accessed | tf_op | source)
XLA Modules:
  0.0 467.6 jit_solution(15775231682070053295)
XLA Ops:
  8.5 0.8 bitcast_select_fusion
  9.3 12.6 %all-to-all-start = ((bf16[32,1,2,8,128]{4,3,2,1,0:T(8,128)(2,1)}), bf16[32,1,2,8,128]{4,3,2,1,0:T(8,128)(2,1)S(1)}, u32[]{:S(2)}, u32[]{:S(2)}) async-start(bf16[32,1,2,8,128]{4,3,2,1,0:T(8,128)(2,1)} %bitcast_select_fusion), calls=%async_computation | async-start | bytes 262144 | tf_op jit(solution)/shard_map/all_to_all | solution.py:112
  23.4 1.0 reshape.231
  24.8 4.3 gather_fusion.1
  29.1 1.9 broadcast_select_fusion
  33.8 1.3 copy.35
  37.9 1.7 fusion.1
  39.6 1.3 convolution_convert_fusion
  40.9 4.6 convolution_bitcast_fusion
  45.5 49.9 %copy.44 = f32[16,8,128,128]{0,1,3,2:T(8,128)} copy(f32[16,8,128,128]{2,3,1,0:T(8,128)} %convolution_bitcast_fusion) | data formatting | bytes 16777216 | tf_op jit(solution)/shard_map/while/body/eval_jaxpr/reshape | solution.py:99
  95.3 33.6 %gather_fusion.6 = f32[2048,16,8]{1,2,0:T(8,128)} fusion(f32[16,8,16384]{0,1,2:T(8,128)} %bitcast.41, s32[2048]{0:T(1024)S(1)} %get-tuple-element.67), kind=kCustom, calls=%fused_computation.3.clone | custom fusion | bytes 2105344 | tf_op jit(solution)/shard_map/while/body/eval_jaxpr/jit(_take)/gather | solution.py:103
  128.9 33.6 %gather_fusion.3 = f32[2048,16,8]{1,2,0:T(8,128)} fusion(f32[16,8,16384]{0,1,2:T(8,128)} %bitcast.41, s32[2048]{0:T(1024)S(1)} %get-tuple-element.57), kind=kCustom, calls=%fused_computation.clone | custom fusion | bytes 2105344 | tf_op jit(solution)/shard_map/while/body/eval_jaxpr/jit(_take)/gather | solution.py:100
  162.6 33.6 %gather_fusion.5 = f32[2048,16,8]{1,2,0:T(8,128)} fusion(f32[16,8,16384]{0,1,2:T(8,128)} %bitcast.41, s32[2048]{0:T(1024)S(1)} %get-tuple-element.56), kind=kCustom, calls=%fused_computation.2.clone | custom fusion | bytes 2105344 | tf_op jit(solution)/shard_map/while/body/eval_jaxpr/jit(_take)/gather | solution.py:103
  196.2 33.5 %gather_fusion.4 = f32[2048,16,8]{1,2,0:T(8,128)} fusion(f32[16,8,16384]{0,1,2:T(8,128)} %bitcast.41, s32[2048]{0:T(1024)S(1)} %get-tuple-element.66), kind=kCustom, calls=%fused_computation.1.clone | custom fusion | bytes 2105344 | tf_op jit(solution)/shard_map/while/body/eval_jaxpr/jit(_take)/gather | solution.py:100
  229.7 21.9 %add_reduce_fusion = (bf16[16,2048]{0,1:T(8,128)(2,1)S(1)}, bf16[16,2048]{0,1:T(8,128)(2,1)S(1)}) fusion(f32[8,2048]{0,1:T(8,128)S(1)} %copy-done.3, f32[8,2048]{0,1:T(8,128)S(1)} %copy.30, f32[2048,16,8]{1,2,0:T(8,128)} %gather_fusion.4, pred[2048]{0:T(1024)(128)(4,1)S(1)} %get-tuple-element.64, f32[2048,16,8]{1,2,0:T(8,128)} %gather_fusion.3, ...), kind=kLoop, calls=%fused_computation.11 | loop fusion | flops 3604480 | bytes 4464640 | tf_op jit(solution)/shard_map/while/body/eval_jaxpr/reduce_sum | solution.py:106
  253.6 74.5 %all-reduce.2.cloned.1.call-done = bf16[1,2,16,2048]{3,2,1,0:T(8,128)(2,1)} async-done(((bf16[1,2,16,2048]{3,2,1,0:T(8,128)(2,1)}), bf16[1,2,16,2048]{3,2,1,0:T(8,128)(2,1)}) %all-reduce.2.cloned.1.call-update) | async-done | bytes 131088 | tf_op jit(solution)/shard_map/psum | solution.py:114
  328.2 0.8 multiply_convert_fusion
  329.0 1.4 fusion.7
  330.3 1.4 fusion.6
  331.9 1.5 copy.46
  333.4 119.0 %reduce-scatter.4.cloned.1.call-done = bf16[8,4096]{1,0:T(8,128)(2,1)} async-done(((bf16[256,4096]{1,0:T(8,128)(2,1)}), bf16[8,4096]{1,0:T(8,128)(2,1)}) %reduce-scatter.4.cloned.1.call-update) | async-done | bytes 65552
  452.3 2.0 reshape.241
  454.4 3.0 copy.40
  457.3 3.4 reshape.240
  (47 shorter events, 8.9 us)
Async XLA Ops:
  6.5 1.4 copy-start
  9.3 28.5 %all-to-all-start = ((bf16[32,1,2,8,128]{4,3,2,1,0:T(8,128)(2,1)}), bf16[32,1,2,8,128]{4,3,2,1,0:T(8,128)(2,1)S(1)}, u32[]{:S(2)}, u32[]{:S(2)}) async-start(bf16[32,1,2,8,128]{4,3,2,1,0:T(8,128)(2,1)} %bitcast_select_fusion), calls=%async_computation | async-start | bytes 262144 | tf_op jit(solution)/shard_map/all_to_all | solution.py:112
  21.8 306.3 %all-reduce.2.cloned.1.call-start = ((), (), s32[]{:S(2)}) async-start(), calls=%async_computation.2 | async-start | bytes 262144 | tf_op jit(solution)/shard_map/psum | solution.py:114
  24.8 6.8 %copy-start.5 = (s32[32]{0:T(128)S(1)}, s32[32]{0:T(128)}, u32[]{:S(2)}) copy-start(s32[32]{0:T(128)} %param.15) | copy-start | bytes 388
  29.1 6.0 %copy-start.2 = (f32[1,32]{1,0:T(1,128)S(1)}, f32[1,32]{1,0:T(1,128)}, u32[]{:S(2)}) copy-start(f32[1,32]{1,0:T(1,128)} %param.12) | copy-start | bytes 388
  29.1 7.9 %copy-start.6 = (f32[32,1]{0,1:T(1,128)S(1)}, f32[32,1]{0,1:T(1,128)}, u32[]{:S(2)}) copy-start(f32[32,1]{0,1:T(1,128)} %param.13) | copy-start | bytes 388
  95.3 134.4 %copy-start.3 = (f32[8,2048]{0,1:T(8,128)S(1)}, f32[8,2048]{0,1:T(8,128)}, u32[]{:S(2)}) copy-start(f32[8,2048]{0,1:T(8,128)} %copy.35) | copy-start | bytes 196612
  229.7 23.2 %copy-start.4 = (s32[1,16]{1,0:T(1,128)S(1)}, s32[1,16]{1,0:T(1,128)}, u32[]{:S(2)}) copy-start(s32[1,16]{1,0:T(1,128)} %param.14) | copy-start | bytes 196
  252.7 199.6 %reduce-scatter.4.cloned.1.call-start = ((), (), s32[]{:S(2)}) async-start(), calls=%async_computation.3 | async-start | bytes 2162688
  452.3 8.4 %copy-start.1 = (bf16[32,1,2,8,128]{4,3,2,1,0:T(8,128)(2,1)S(1)}, bf16[32,1,2,8,128]{4,3,2,1,0:T(8,128)(2,1)}, u32[]{:S(2)}) copy-start(bf16[32,1,2,8,128]{4,3,2,1,0:T(8,128)(2,1)} %param.11) | copy-start | bytes 393220
Sparse Core Ops, SparseCore 0:
  252.8 75.2 all-reduce.1
  333.5 118.7 reduce-scatter.3
where the time goes:
time: 475 us; the launch traced here: 468 us
  local copies, waits for them, and re-layouts  204 us (43%)
  waiting for transfers between devices  194 us (41%)
  other arithmetic  32.1 us (7%)
  between operations  16.2 us (3%)
  starting transfers between devices  12.8 us (3%)
  matrix products  8.6 us (2%)
    unnamed x3, waiting for transfers between devices  119 us
    psum x1, waiting for transfers between devices, shards(): summed = lax.psum(partial_value.astype(jnp.bfloat16), 'band')  74.5 us
    reshape x1, local copies, waits for them, and re-layouts, item_terms(): flat_view = mixed_part.reshape(selected_count, slab_width, twice * twice)  49.9 us
    gather x1, local copies, waits for them, and re-layouts, item_terms(): jnp.take(flat_view, first_index, axis=2)  33.6 us
    gather x1, local copies, waits for them, and re-layouts, item_terms(): jnp.take(flat_view, third_index, axis=2)  33.6 us
    gather x1, local copies, waits for them, and re-layouts, item_terms(): jnp.take(flat_view, fourth_index, axis=2)  33.6 us
    gather x1, local copies, waits for them, and re-layouts, item_terms(): jnp.take(flat_view, second_index, axis=2)  33.5 us
    reduce_sum x1, other arithmetic, item_terms(): jnp.sum(plane_cos[None] * real_cols + plane_sin[None] * imag_cols, axis=1)  21.9 us
  transfers between devices with their start and end apart: 3, of which 2 were waited for; matrix products, arithmetic and copies ran while one was open for 3% of the time, Pallas kernels for 0%

commit v1 on v0

v1 whole, which is shorter than its diff:
```python
import math

import jax
import jax.numpy as jnp
import numpy as np
from jax import lax
from jax.experimental import pallas as pl
from jax.experimental.pallas import tpu as pltpu
from jax.sharding import Mesh
from jax.sharding import PartitionSpec as P

GRID = 64
HALF = 32
NG = 2048
NOCC = 16
SLAB = 8
AXES = ("xh", "z", "c", "xl", "y")
KA = ("xh", "z", "c")
BAND = ("xl", "y")


def tables():
    pos = np.arange(GRID)
    freq = np.arange(HALF) - HALF // 2
    ang = (freq[:, None] * pos[None, :] % GRID) * (2.0 * math.pi / GRID)
    cos, sin = np.cos(ang), np.sin(ang)
    eye = np.eye(SLAB)
    ymat = np.stack([cos, sin])
    ymat = np.einsum("wgy,xu->wgxyu", ymat, eye).reshape(2 * HALF * SLAB, GRID * SLAB)
    ct, st = cos.T, sin.T
    zre = np.concatenate([ct, -st, -st, -ct], axis=0)
    zim = np.concatenate([-st, -ct, -ct, st], axis=0)
    zmat = np.zeros((4, 4 * GRID, 2, 4, HALF))
    for g in range(4):
        zmat[g, :, 0, g] = zre
        zmat[g, :, 1, g] = zim
    zmat = zmat.reshape(1024, 256)
    scale = float(GRID) ** -1.5
    xtab = np.concatenate(
        [cos.T.reshape(8, SLAB, HALF), sin.T.reshape(8, SLAB, HALF)], axis=1
    ) * scale
    hi = xtab.astype(jnp.bfloat16).astype(np.float64)
    xtab = np.concatenate([hi, xtab - hi], axis=2)
    pick = np.zeros((8, 2, 2, 2, 2, 2, NOCC, SLAB))
    for b in range(8):
        for h in range(2):
            for j in range(2):
                for c in range(2):
                    pick[b, h, j, c, h, c, 2 * b + j, :] = 1.0
    pick = pick.reshape(64, 512)
    return [np.asarray(a, np.float32).astype(jnp.bfloat16) for a in (ymat, zmat, xtab, pick)]


def density_kernel(sel, val, cond, waves, ymat, zmat, xtab, pick, out,
                   vbuf, c1, c2, pbuf, gbuf, fbuf, cosb, sinb, sems):
    copies = [
        pltpu.make_async_copy(val.at[0, sel[0, j]], vbuf.at[j], sems.at[j])
        for j in range(NOCC)
    ]
    for copy in copies:
        copy.start()
    low = lax.broadcasted_iota(jnp.int32, (512, 128), 1) < GRID
    cf = cond[...].reshape(512, 128).astype(jnp.float32)
    cr = pltpu.roll(cf, GRID, 1)
    c1[...] = jnp.where(low, cf, cr)
    c2[...] = jnp.where(low, cr, -cf)

    gx = waves[0:1, :] + HALF // 2
    hot = (lax.broadcasted_iota(jnp.int32, (2 * HALF, NG), 0) % HALF == gx)
    hot = hot.astype(jnp.float32).astype(jnp.bfloat16)
    phase = jnp.dot(xtab[...], hot, preferred_element_type=jnp.float32)
    cosb[...] = phase[:SLAB]
    sinb[...] = phase[SLAB:]

    for copy in copies:
        copy.wait()

    def y_step(p, carry):
        for q in range(2):
            v = vbuf[2 * p + q].reshape(512, 128).astype(jnp.float32)
            pair = v * c1[...] + pltpu.roll(v, GRID, 1) * c2[...]
            pbuf[:, 128 * q:128 * (q + 1)] = pair.astype(jnp.bfloat16)
        g = jnp.dot(ymat[...], pbuf[...], preferred_element_type=jnp.float32)
        g = g.reshape(2, HALF, SLAB, 256)
        g = jnp.concatenate([g[..., :128], g[..., 128:]], axis=2).astype(jnp.bfloat16)
        for w in range(2):
            for gy in range(HALF):
                row = pl.multiple_of((gy // 4) * 128 + p * 16, 16)
                lane = ((gy % 4) * 2 + w) * 128
                gbuf[pl.ds(row, 16), lane:lane + 128] = g[w, gy]
        return carry

    lax.fori_loop(0, NOCC // 2, y_step, 0)

    for n in range(4):
        f = jnp.dot(gbuf[256 * n:256 * (n + 1), :], zmat[...], preferred_element_type=jnp.float32)
        f = f.astype(jnp.bfloat16)
        for k in range(2):
            lane = (2 * n + k) * 128
            fbuf[0:128, lane:lane + 128] = f[128 * k:128 * (k + 1), :128]
            fbuf[128:256, lane:lane + 128] = f[128 * k:128 * (k + 1), 128:]

    def t_step(n, carry):
        parts = []
        for h in range(2):
            lane = pl.multiple_of(n * 256 + h * 1024, 256)
            idx = (waves[1:2, pl.ds(lane, 256)] + HALF // 2) * HALF + (
                waves[2:3, pl.ds(lane, 256)] + HALF // 2
            )
            onehot = lax.broadcasted_iota(jnp.int32, (1024, 256), 0) == idx
            onehot = onehot.astype(jnp.float32).astype(jnp.bfloat16)
            f = jnp.dot(fbuf[...], onehot, preferred_element_type=jnp.float32)
            fr = f[:128].reshape(NOCC, SLAB, 256)
            fi = f[128:].reshape(NOCC, SLAB, 256)
            cs = cosb[:, pl.ds(lane, 256)][None]
            sn = sinb[:, pl.ds(lane, 256)][None]
            parts.append((cs * fr + sn * fi).astype(jnp.bfloat16).reshape(128, 256))
            parts.append((cs * fi - sn * fr).astype(jnp.bfloat16).reshape(128, 256))
        total = jnp.dot(pick[...], jnp.concatenate(parts, axis=0), preferred_element_type=jnp.float32)
        dst = pl.multiple_of(n * 256, 256)
        out[:, :, pl.ds(dst, 256)] = total.astype(jnp.bfloat16).reshape(8, 8, 256)
        return carry

    lax.fori_loop(0, 4, t_step, 0)


def pack_kernel(band, partner, sel, val_e, cond_e, freq, recv, out):
    total = jnp.sum(recv[...].astype(jnp.float32), axis=0).astype(jnp.bfloat16).astype(jnp.float32)
    e = cond_e[partner[0], 0]
    b = band[0]
    d0 = val_e[0, sel[0, 2 * b]] - e
    d1 = val_e[0, sel[0, 2 * b + 1]] - e
    rows = lax.broadcasted_iota(jnp.int32, (8, 128), 0)
    gap = jnp.where((rows // 2) % 2 == 0, d0, d1)
    w = freq[0]
    weight = 2.0 * gap / (gap * gap + w * w) / 512.0
    for z in range(8):
        wt = weight * total[:, 128 * z:128 * (z + 1)]
        for t in range(8):
            out[z * 8 + t] = jnp.concatenate(
                [wt, total[:, 128 * t:128 * (t + 1)]], axis=0
            ).astype(jnp.bfloat16)


def chi_kernel(recv, out, buf):
    buf[...] = recv[...].astype(jnp.float32).reshape(1024, 128)

    def rows(kind, h, j, c):
        return buf[pl.ds(8 * kind + 4 * h + 2 * j + c, 64, stride=16), :]

    right = jnp.concatenate(
        [
            jnp.concatenate([rows(1, h, j, c) for c in range(2) for j in range(2)], axis=0)
            for h in range(2)
        ],
        axis=1,
    ).astype(jnp.bfloat16)
    dims = (((0,), (0,)), ((), ()))
    for h in range(2):
        re = [rows(0, h, j, 0) for j in range(2)]
        im = [rows(0, h, j, 1) for j in range(2)]
        left = jnp.concatenate(
            [jnp.concatenate(re + im, axis=0), jnp.concatenate(im + [-r for r in re], axis=0)],
            axis=1,
        ).astype(jnp.bfloat16)
        chi = lax.dot_general(left, right, dims, preferred_element_type=jnp.float32)
        chi = jnp.concatenate(
            [chi[:128].reshape(16, 8, 256), chi[128:].reshape(16, 8, 256)], axis=1
        )
        out[16 * h:16 * (h + 1)] = chi.astype(jnp.bfloat16)


def final_kernel(recv, out):
    for b in range(8):
        acc = recv[b].astype(jnp.float32)
        for s in range(1, 4):
            acc = acc + recv[8 * s + b].astype(jnp.float32)
        for h in range(2):
            lane = h * 1024 + b * 128
            out[0, :, lane:lane + 128] = acc[:8, 128 * h:128 * (h + 1)]
            out[1, :, lane:lane + 128] = acc[8:, 128 * h:128 * (h + 1)]


VM = pl.BlockSpec(memory_space=pltpu.VMEM)
SM = pl.BlockSpec(memory_space=pltpu.SMEM)


def shards(
    valence_orbitals,
    conduction_orbitals,
    valence_energy,
    conduction_energy,
    valence_select,
    shifted_index,
    wave_vectors,
    frequency,
):
    ymat, zmat, xtab, pick = tables()
    band = lax.axis_index(BAND)
    partner = lax.dynamic_slice_in_dim(shifted_index, lax.axis_index(KA), 1)
    ordered = conduction_orbitals[:, 0].at[shifted_index].get(mode="promise_in_bounds")
    cond = lax.all_to_all(ordered, KA, split_axis=0, concat_axis=0, tiled=True)
    xown = lax.dynamic_index_in_dim(jnp.asarray(xtab), band, 0, keepdims=False)
    f32, bf16 = jnp.float32, jnp.bfloat16
    partial = pl.pallas_call(
        density_kernel,
        out_shape=jax.ShapeDtypeStruct((8, 8, 1024), bf16),
        in_specs=[SM, pl.BlockSpec(memory_space=pl.ANY)] + [VM] * 6,
        out_specs=VM,
        scratch_shapes=[
            pltpu.VMEM((NOCC, GRID, SLAB, 128), bf16),
            pltpu.VMEM((512, 128), f32),
            pltpu.VMEM((512, 128), f32),
            pltpu.VMEM((512, 256), bf16),
            pltpu.VMEM((1024, 1024), bf16),
            pltpu.VMEM((256, 1024), bf16),
            pltpu.VMEM((SLAB, NG), f32),
            pltpu.VMEM((SLAB, NG), f32),
            pltpu.SemaphoreType.DMA((NOCC,)),
        ],
        name="density",
    )(valence_select, valence_orbitals, cond, wave_vectors, ymat, zmat, xown, pick)
    recv = lax.all_to_all(partial, BAND, split_axis=0, concat_axis=0, tiled=True)
    packed = pl.pallas_call(
        pack_kernel,
        out_shape=jax.ShapeDtypeStruct((64, 16, 128), bf16),
        in_specs=[SM] * 6 + [VM],
        out_specs=VM,
        name="pack",
    )(band[None], partner, valence_select, valence_energy, conduction_energy, frequency, recv)
    recv = lax.all_to_all(packed, ("z",) + BAND, split_axis=0, concat_axis=0, tiled=True)
    chi = pl.pallas_call(
        chi_kernel,
        out_shape=jax.ShapeDtypeStruct((32, 16, 256), bf16),
        in_specs=[VM],
        out_specs=VM,
        scratch_shapes=[pltpu.VMEM((1024, 128), f32)],
        name="chi",
    )(recv)
    recv = lax.all_to_all(chi, ("xh", "c") + BAND, split_axis=0, concat_axis=0, tiled=True)
    return pl.pallas_call(
        final_kernel,
        out_shape=jax.ShapeDtypeStruct((2, 8, NG), f32),
        in_specs=[VM],
        out_specs=VM,
        name="final",
    )(recv)


def solution(mesh):
    fine = Mesh(mesh.devices.reshape(2, 8, 2, 2, 4), AXES)
    in_specs = (
        P(KA, None, None, BAND, None),
        P(None, None, KA, BAND, None),
        P(KA, None),
        P(),
        P(KA, None),
        P(),
        P(),
        P(),
    )
    out_specs = P(None, AXES, None)
    return jax.shard_map(shards, mesh=fine, in_specs=in_specs, out_specs=out_specs, check_vma=False)
```

time: 475 us -> 86.6 us (0.18); the launches traced: 468 us -> 86 us
  local copies, waits for them, and re-layouts: 204 us -> 5.29 us
  waiting for transfers between devices: 194 us -> 12.7 us
  blocking collectives: 0 us -> 33.5 us
  other arithmetic: 32.1 us -> 0.73 us
  Pallas kernels: 0 us -> 16.3 us
  between operations: 16.2 us -> 0.7 us
  matrix products: 8.6 us -> 0 us
    gather x7 -> x1, local copies, waits for them, and re-layouts: 140 us -> 1.24 us  [shards(): conduction_orbitals[:, 0].at[shifted_index].get(mode='promise_in_bounds')]
    unnamed x3 -> x0, waiting for transfers between devices: 119 us -> none
    psum x1 -> x0, waiting for transfers between devices: 74.5 us -> none  [shards(): summed = lax.psum(partial_value.astype(jnp.bfloat16), 'band')]
    reshape x3 -> x0, local copies, waits for them, and re-layouts: 51.1 us -> none  [the longest x1 49.9 us: item_terms(): flat_view = mixed_part.reshape(selected_count, slab_width, twice * twice)]
    all_to_all x0 -> x2, blocking collectives: none -> 33.5 us  [the longest x1 17.5 us: shards(): lax.all_to_all(chi, ('xh', 'c') + BAND, split_axis=0, concat_axis=0, tile...]
    reduce_sum x1 -> x0, other arithmetic: 21.9 us -> none  [item_terms(): jnp.sum(plane_cos[None] * real_cols + plane_sin[None] * imag_cols, axis=1)]
    pallas_call x0 -> x4, Pallas kernels: none -> 16.3 us  [the longest x1 10.4 us: shards(): pl.pallas_call(density_kernel, out_shape=jax.ShapeDtypeStruct((8, 8, 1024...]
    all_to_all x1 -> x2, waiting for transfers between devices: 0.01 us -> 12.7 us  [the longest x1 9.2 us: shards(): cond = lax.all_to_all(ordered, KA, split_axis=0, concat_axis=0, tiled=True)]
  transfers between devices with their start and end apart: 3 -> 2, of which waited for: 2 -> 2; matrix products, arithmetic and copies ran while one was open for 3% -> 3% of each run, Pallas kernels for 0% -> 0%
where the time goes in v1:
time: 86.6 us; the launch traced here: 86 us
  blocking collectives  33.5 us (39%)
  starting transfers between devices  16.8 us (19%)
  Pallas kernels  16.3 us (19%)
  waiting for transfers between devices  12.7 us (15%)
  local copies, waits for them, and re-layouts  5.29 us (6%)
    all_to_all x1, blocking collectives, shards(): lax.all_to_all(chi, ('xh', 'c') + BAND, split_axis=0, concat_axis=0, tile...  17.5 us
    all_to_all x1, blocking collectives, shards(): lax.all_to_all(packed, ('z',) + BAND, split_axis=0, concat_axis=0, tiled=...  16 us
    all_to_all x1, starting transfers between devices, shards(): cond = lax.all_to_all(ordered, KA, split_axis=0, concat_axis=0, tiled=True)  12.6 us
    pallas_call x1, Pallas kernels, shards(): pl.pallas_call(density_kernel, out_shape=jax.ShapeDtypeStruct((8, 8, 1024...  10.4 us
    all_to_all x1, waiting for transfers between devices, shards(): cond = lax.all_to_all(ordered, KA, split_axis=0, concat_axis=0, tiled=True)  9.2 us
    all_to_all x1, starting transfers between devices, shards(): lax.all_to_all(partial, BAND, split_axis=0, concat_axis=0, tiled=True)  4.24 us
    all_to_all x1, waiting for transfers between devices, shards(): lax.all_to_all(partial, BAND, split_axis=0, concat_axis=0, tiled=True)  3.5 us
    pallas_call x1, Pallas kernels, shards(): pl.pallas_call(pack_kernel, out_shape=jax.ShapeDtypeStruct((64, 16, 128),...  2.25 us
  transfers between devices with their start and end apart: 2, of which 2 were waited for; matrix products, arithmetic and copies ran while one was open for 3% of the time, Pallas kernels for 0%

profile of v1, /device:TPU:1, one launch (start us, length us, event | category | flops | bytes accessed | tf_op | source)
XLA Modules:
  0.0 86.0 jit_solution(2893675718351401347)
XLA Ops:
  0.0 0.0 copy-start
  0.0 0.0 copy-start.4
  0.0 0.0 copy-start.3
  0.0 0.7 compare_select_fusion
  0.7 0.2 copy-done
  0.9 1.2 %gather_fusion = bf16[32,2,8,128]{3,2,1,0:T(8,128)(2,1)} fusion(bf16[32,2,8,128]{3,2,1,0:T(8,128)(2,1)S(1)} %bitcast.4, s32[1024]{0:T(1024)S(1)} %pad_clamp_fusion), kind=kCustom, calls=%fused_computation | custom fusion | bytes 262272 | tf_op jit(solution)/shard_map/gather | solution.py:201
  2.2 12.6 %all-to-all-start = ((bf16[32,2,8,128]{3,2,1,0:T(8,128)(2,1)}), bf16[32,2,8,128]{3,2,1,0:T(8,128)(2,1)S(1)}, u32[]{:S(2)}, u32[]{:S(2)}) async-start(bf16[32,2,8,128]{3,2,1,0:T(8,128)(2,1)} %gather_fusion), calls=%async_computation | async-start | bytes 262144 | tf_op jit(solution)/shard_map/all_to_all | solution.py:202
  14.7 1.3 %dynamic-slice_bitcast_fusion.xtab = bf16[16,64]{1,0:T(8,128)(2,1)} fusion(bf16[8,16,64]{2,1,0:T(8,128)(2,1)} %constant.45.clone, s32[]{:T(128)S(6)} %select_n.12), kind=kLoop, calls=%fused_computation.2 | loop fusion | bytes 4100 | tf_op jit(solution)/shard_map/jit(dynamic_index_in_dim)/squeeze | solution.py:203
  16.0 9.2 %all-to-all-done.cond = bf16[32,2,8,128]{3,2,1,0:T(8,128)(2,1)S(1)} async-done(((bf16[32,2,8,128]{3,2,1,0:T(8,128)(2,1)}), bf16[32,2,8,128]{3,2,1,0:T(8,128)(2,1)S(1)}, u32[]{:S(2)}, u32[]{:S(2)}) %all-to-all-start) | async-done | bytes 131104 | tf_op jit(solution)/shard_map/all_to_all | solution.py:202
  25.2 0.0 copy-start.1
  25.2 0.7 copy-done.1
  25.9 10.4 %density.1 = bf16[8,8,1024]{2,1,0:T(8,128)(2,1)} custom-call(s32[1,16]{1,0:T(1,128)} %sel.3, bf16[1,32,64,8,128]{4,3,2,1,0:T(8,128)(2,1)} %val.1, bf16[32,2,8,128]{3,2,1,0:T(8,128)(2,1)} %copy-done.1, s32[3,2048]{1,0:T(4,128)} %waves.1, bf16[512,512]{1,0:T(8,128)(2,1)} %constant.46.clone.ymat, bf16[1024,256]{1,0:T(8,128)(2,1)} %constant.47.clone.zmat, ...), custom_call_target="tpu_custom_call" | custom-call | tf_op jit(solution)/shard_map/density/pallas_call | solution.py:205
  36.3 4.2 %all-to-all-start.1 = ((bf16[8,8,1024]{2,1,0:T(8,128)(2,1)}), bf16[8,8,1024]{2,1,0:T(8,128)(2,1)S(1)}, u32[]{:S(2)}, u32[]{:S(2)}) async-start(bf16[8,8,1024]{2,1,0:T(8,128)(2,1)} %density.1), calls=%async_computation.1 | async-start | bytes 262144 | tf_op jit(solution)/shard_map/all_to_all | solution.py:223
  41.2 0.0 copy-done.4
  41.2 0.6 dynamic_slice.7.partner
  41.8 0.0 copy-done.3
  41.8 0.7 copy.13.cond_e
  42.5 3.5 %all-to-all-done.1.recv = bf16[8,8,1024]{2,1,0:T(8,128)(2,1)S(1)} async-done(((bf16[8,8,1024]{2,1,0:T(8,128)(2,1)}), bf16[8,8,1024]{2,1,0:T(8,128)(2,1)S(1)}, u32[]{:S(2)}, u32[]{:S(2)}) %all-to-all-start.1) | async-done | bytes 131104 | tf_op jit(solution)/shard_map/all_to_all | solution.py:223
  46.0 0.7 copy-done.2
  46.6 2.2 %pack.1 = bf16[64,16,128]{2,1,0:T(8,128)(2,1)} custom-call(s32[1]{0:T(128)} %bitcast.band, s32[1]{0:T(128)} %dynamic_slice.7.partner, s32[1,16]{1,0:T(1,128)} %sel.3, f32[1,32]{1,0:T(1,128)} %val_e.1, f32[32,1]{1,0:T(8,128)} %copy.13.cond_e, f32[1]{0:T(128)S(6)} %copy.14.freq, bf16[8,8,1024]{2,1,0:T(8,128)(2,1)} %copy-done.2), custom_call_target="tpu_custom_call" | custom-call | tf_op jit(solution)/shard_map/pack/pallas_call | solution.py:224
  48.9 16.0 %all_to_all.20.recv = bf16[64,16,128]{2,1,0:T(8,128)(2,1)} all-to-all(bf16[64,16,128]{2,1,0:T(8,128)(2,1)} %pack.1), channel_id=1, replica_groups=mesh['xh'=2,'z'=8,'c'=2,'xl'=2,'y'=4] {'z','xl','y'}, dimensions={0} | all-to-all | bytes 524288 | tf_op jit(solution)/shard_map/all_to_all | solution.py:231
  64.9 2.0 %chi.1 = bf16[32,16,256]{2,1,0:T(8,128)(2,1)} custom-call(bf16[64,16,128]{2,1,0:T(8,128)(2,1)} %all_to_all.20.recv), custom_call_target="tpu_custom_call" | custom-call | tf_op jit(solution)/shard_map/chi/pallas_call | solution.py:232
  66.9 17.5 %all_to_all.21.recv = bf16[32,16,256]{2,1,0:T(8,128)(2,1)} all-to-all(bf16[32,16,256]{2,1,0:T(8,128)(2,1)} %chi.1), channel_id=1, replica_groups=mesh['xh'=2,'z'=8,'c'=2,'xl'=2,'y'=4] {'xh','c','xl','y'}, dimensions={0} | all-to-all | bytes 524288 | tf_op jit(solution)/shard_map/all_to_all | solution.py:240
  84.4 1.6 %final.1 = f32[2,8,2048]{2,1,0:T(8,128)} custom-call(bf16[32,16,256]{2,1,0:T(8,128)(2,1)} %all_to_all.21.recv), custom_call_target="tpu_custom_call" | custom-call | tf_op jit(solution)/shard_map/final/pallas_call | solution.py:241
  (2 shorter events, 0.0 us)
Async XLA Ops:
  0.0 0.9 %copy-start = (bf16[32,1,2,8,128]{4,3,2,1,0:T(8,128)(2,1)S(1)}, bf16[32,1,2,8,128]{4,3,2,1,0:T(8,128)(2,1)}, u32[]{:S(2)}) copy-start(bf16[32,1,2,8,128]{4,3,2,1,0:T(8,128)(2,1)} %param.13) | copy-start | bytes 393220
  0.0 41.2 %copy-start.4 = (s32[32]{0:T(128)S(1)}, s32[32]{0:T(128)}, u32[]{:S(2)}) copy-start(s32[32]{0:T(128)} %param.17) | copy-start | bytes 388
  0.0 41.8 %copy-start.3 = (f32[32,1]{0,1:T(1,128)S(1)}, f32[32,1]{0,1:T(1,128)}, u32[]{:S(2)}) copy-start(f32[32,1]{0,1:T(1,128)} %param.15) | copy-start | bytes 388
  2.2 23.1 %all-to-all-start = ((bf16[32,2,8,128]{3,2,1,0:T(8,128)(2,1)}), bf16[32,2,8,128]{3,2,1,0:T(8,128)(2,1)S(1)}, u32[]{:S(2)}, u32[]{:S(2)}) async-start(bf16[32,2,8,128]{3,2,1,0:T(8,128)(2,1)} %gather_fusion), calls=%async_computation | async-start | bytes 262144 | tf_op jit(solution)/shard_map/all_to_all | solution.py:202
  25.2 0.7 copy-start.1
  36.3 9.7 %all-to-all-start.1 = ((bf16[8,8,1024]{2,1,0:T(8,128)(2,1)}), bf16[8,8,1024]{2,1,0:T(8,128)(2,1)S(1)}, u32[]{:S(2)}, u32[]{:S(2)}) async-start(bf16[8,8,1024]{2,1,0:T(8,128)(2,1)} %density.1), calls=%async_computation.1 | async-start | bytes 262144 | tf_op jit(solution)/shard_map/all_to_all | solution.py:223
  46.0 0.7 copy-start.2

commit v2 on v1

v2 whole, which is shorter than its diff:
```python
import math

import jax
import jax.numpy as jnp
import numpy as np
from jax import lax
from jax.experimental import pallas as pl
from jax.experimental.pallas import tpu as pltpu
from jax.sharding import Mesh
from jax.sharding import PartitionSpec as P

GRID = 64
HALF = 32
NG = 2048
NOCC = 16
SLAB = 8
AXES = ("xh", "z", "c", "xl", "y")
KA = ("xh", "z", "c")
BAND = ("xl", "y")


def tables():
    pos = np.arange(GRID)
    freq = np.arange(HALF) - HALF // 2
    ang = (freq[:, None] * pos[None, :] % GRID) * (2.0 * math.pi / GRID)
    cos, sin = np.cos(ang), np.sin(ang)
    eye = np.eye(SLAB)
    ymat = np.stack([cos, sin])
    ymat = np.einsum("wgy,xu->wgxyu", ymat, eye).reshape(2 * HALF * SLAB, GRID * SLAB)
    ct, st = cos.T, sin.T
    zre = np.concatenate([ct, -st, -st, -ct], axis=0)
    zim = np.concatenate([-st, -ct, -ct, st], axis=0)
    zmat = np.zeros((4, 4 * GRID, 2, 4, HALF))
    for g in range(4):
        zmat[g, :, 0, g] = zre
        zmat[g, :, 1, g] = zim
    zmat = zmat.reshape(1024, 256)
    scale = float(GRID) ** -1.5
    xtab = np.concatenate(
        [cos.T.reshape(8, SLAB, HALF), sin.T.reshape(8, SLAB, HALF)], axis=1
    ) * scale
    hi = xtab.astype(jnp.bfloat16).astype(np.float64)
    xtab = np.concatenate([hi, xtab - hi], axis=2)
    pick = np.zeros((8, 2, 2, 2, 2, 2, NOCC, SLAB))
    for b in range(8):
        for h in range(2):
            for j in range(2):
                for c in range(2):
                    pick[b, h, j, c, h, c, 2 * b + j, :] = 1.0
    pick = pick.reshape(64, 512)
    return [np.asarray(a, np.float32).astype(jnp.bfloat16) for a in (ymat, zmat, xtab, pick)]


def order_kernel(shift, cond, out, idx, rows, sems):
    one = pltpu.make_async_copy(shift, idx, sems.at[0])
    two = pltpu.make_async_copy(cond, rows, sems.at[1])
    one.start()
    two.start()
    one.wait()
    two.wait()
    for k in range(32):
        out[k] = rows[idx[k], 0]


def prep_kernel(ids, sel_h, shift_h, vale_h, conde_h, freq_h, waves_h, xtab_h, phase, weight,
                sel, shift, val_e, cond_e, freq, waves, xtab, sems):
    pairs = [
        (sel_h, sel),
        (xtab_h.at[ids[1]], xtab),
        (waves_h, waves),
        (shift_h, shift),
        (vale_h, val_e),
        (conde_h, cond_e),
        (freq_h, freq),
    ]
    copies = [pltpu.make_async_copy(a, b, sems.at[i]) for i, (a, b) in enumerate(pairs)]
    for copy in copies:
        copy.start()
    for copy in copies:
        copy.wait()
    gx = waves[0:1, :] + HALF // 2
    hot = (lax.broadcasted_iota(jnp.int32, (2 * HALF, NG), 0) % HALF == gx)
    hot = hot.astype(jnp.float32).astype(jnp.bfloat16)
    phase[...] = jnp.dot(xtab[...], hot, preferred_element_type=jnp.float32)
    e = cond_e[shift[ids[0]]]
    d0 = val_e[0, sel[0, 2 * ids[1]]] - e
    d1 = val_e[0, sel[0, 2 * ids[1] + 1]] - e
    rows = lax.broadcasted_iota(jnp.int32, (8, 128), 0)
    gap = jnp.where((rows // 2) % 2 == 0, d0, d1)
    w = freq[0]
    weight[...] = 2.0 * gap / (gap * gap + w * w) / 512.0


def density_kernel(sel, val, phase, cond, waves, ymat, zmat, pick, out, vbuf, c1, c2, pbuf, gbuf, fbuf, sems):
    copies = [
        pltpu.make_async_copy(val.at[0, sel[0, j]], vbuf.at[j], sems.at[j])
        for j in range(NOCC)
    ]
    for copy in copies:
        copy.start()
    low = lax.broadcasted_iota(jnp.int32, (512, 128), 1) < GRID
    cf = cond[...].reshape(512, 128).astype(jnp.float32)
    cr = pltpu.roll(cf, GRID, 1)
    c1[...] = jnp.where(low, cf, cr).astype(jnp.bfloat16)
    c2[...] = jnp.where(low, cr, -cf).astype(jnp.bfloat16)
    for copy in copies:
        copy.wait()

    for p in range(NOCC // 2):
        for q in range(2):
            j = 2 * p + q
            v = vbuf[j].reshape(512, 128)
            pair = v * c1[...] + pltpu.roll(v, GRID, 1) * c2[...]
            pbuf[p % 2, :, 128 * q:128 * (q + 1)] = pair
        g = jnp.dot(ymat[...], pbuf[p % 2], preferred_element_type=jnp.float32)
        g = g.reshape(2, HALF, SLAB, 256)
        g = jnp.concatenate([g[..., :128], g[..., 128:]], axis=2).astype(jnp.bfloat16)
        for w in range(2):
            for gy in range(HALF):
                row = (gy // 4) * 128 + p * 16
                lane = ((gy % 4) * 2 + w) * 128
                gbuf[row:row + 16, lane:lane + 128] = g[w, gy]

    f = jnp.dot(gbuf[...], zmat[...], preferred_element_type=jnp.float32).astype(jnp.bfloat16)
    for k in range(8):
        fbuf[0:128, 128 * k:128 * (k + 1)] = f[128 * k:128 * (k + 1), :128]
        fbuf[128:256, 128 * k:128 * (k + 1)] = f[128 * k:128 * (k + 1), 128:]

    for n in range(4):
        parts = []
        for h in range(2):
            lane = n * 256 + h * 1024
            idx = (waves[1:2, lane:lane + 256] + HALF // 2) * HALF + (
                waves[2:3, lane:lane + 256] + HALF // 2
            )
            onehot = lax.broadcasted_iota(jnp.int32, (1024, 256), 0) == idx
            onehot = onehot.astype(jnp.float32).astype(jnp.bfloat16)
            f = jnp.dot(fbuf[...], onehot, preferred_element_type=jnp.float32)
            fr = f[:128].reshape(NOCC, SLAB, 256)
            fi = f[128:].reshape(NOCC, SLAB, 256)
            cs = phase[:SLAB, lane:lane + 256][None]
            sn = phase[SLAB:, lane:lane + 256][None]
            parts.append((cs * fr + sn * fi).astype(jnp.bfloat16).reshape(128, 256))
            parts.append((cs * fi - sn * fr).astype(jnp.bfloat16).reshape(128, 256))
        total = jnp.dot(pick[...], jnp.concatenate(parts, axis=0), preferred_element_type=jnp.float32)
        out[:, :, n * 256:(n + 1) * 256] = total.astype(jnp.bfloat16).reshape(8, 8, 256)


def pack_kernel(weight, recv, out):
    total = jnp.sum(recv[...].astype(jnp.float32), axis=0).astype(jnp.bfloat16).astype(jnp.float32)
    w = weight[...]
    for z in range(8):
        wt = w * total[:, 128 * z:128 * (z + 1)]
        for t in range(8):
            out[z * 8 + t] = jnp.concatenate(
                [wt, total[:, 128 * t:128 * (t + 1)]], axis=0
            ).astype(jnp.bfloat16)


def chi_kernel(recv, out, buf):
    buf[...] = recv[...].astype(jnp.float32).reshape(1024, 128)

    def rows(kind, h, j, c):
        return buf[pl.ds(8 * kind + 4 * h + 2 * j + c, 64, stride=16), :]

    right = jnp.concatenate(
        [
            jnp.concatenate([rows(1, h, j, c) for c in range(2) for j in range(2)], axis=0)
            for h in range(2)
        ],
        axis=1,
    ).astype(jnp.bfloat16)
    dims = (((0,), (0,)), ((), ()))
    for h in range(2):
        re = [rows(0, h, j, 0) for j in range(2)]
        im = [rows(0, h, j, 1) for j in range(2)]
        left = jnp.concatenate(
            [jnp.concatenate(re + im, axis=0), jnp.concatenate(im + [-r for r in re], axis=0)],
            axis=1,
        ).astype(jnp.bfloat16)
        chi = lax.dot_general(left, right, dims, preferred_element_type=jnp.float32)
        chi = jnp.concatenate(
            [chi[:128].reshape(16, 8, 256), chi[128:].reshape(16, 8, 256)], axis=1
        )
        out[16 * h:16 * (h + 1)] = chi.astype(jnp.bfloat16)


def final_kernel(recv, out):
    for b in range(8):
        acc = recv[b].astype(jnp.float32)
        for s in range(1, 4):
            acc = acc + recv[8 * s + b].astype(jnp.float32)
        for h in range(2):
            lane = h * 1024 + b * 128
            out[0, :, lane:lane + 128] = acc[:8, 128 * h:128 * (h + 1)]
            out[1, :, lane:lane + 128] = acc[8:, 128 * h:128 * (h + 1)]


VM = pl.BlockSpec(memory_space=pltpu.VMEM)
SM = pl.BlockSpec(memory_space=pltpu.SMEM)
HB = pl.BlockSpec(memory_space=pltpu.HBM)
F32, BF16 = jnp.float32, jnp.bfloat16


def call(kernel, name, shapes, specs, scratch=(), mib=4, cost=None):
    many = isinstance(shapes, list)
    structs = [
        pltpu.VMEM(s, d) if many else jax.ShapeDtypeStruct(s, d)
        for s, d in (shapes if many else [shapes])
    ]
    return pl.pallas_call(
        kernel,
        out_shape=structs if many else structs[0],
        in_specs=specs,
        out_specs=[VM] * len(structs) if many else VM,
        scratch_shapes=list(scratch),
        compiler_params=pltpu.CompilerParams(vmem_limit_bytes=mib << 20),
        cost_estimate=cost,
        name=name,
    )


def shards(
    valence_orbitals,
    conduction_orbitals,
    valence_energy,
    conduction_energy,
    valence_select,
    shifted_index,
    wave_vectors,
    frequency,
):
    ymat, zmat, xtab, pick = tables()
    ids = jnp.stack([lax.axis_index(KA), lax.axis_index(BAND)])
    ordered = call(
        order_kernel,
        "order",
        ((32, 2, SLAB, 128), BF16),
        [HB, HB],
        [
            pltpu.SMEM((32,), jnp.int32),
            pltpu.VMEM((32, 1, 2, SLAB, 128), BF16),
            pltpu.SemaphoreType.DMA((2,)),
        ],
        mib=63,
    )(shifted_index, conduction_orbitals)
    cond = lax.all_to_all(ordered, KA, split_axis=0, concat_axis=0, tiled=True)
    phase, weight = call(
        prep_kernel,
        "prep",
        [((16, NG), F32), ((8, 128), F32)],
        [SM] + [HB] * 7,
        [
            pltpu.SMEM((1, NOCC), jnp.int32),
            pltpu.SMEM((32,), jnp.int32),
            pltpu.SMEM((1, 32), F32),
            pltpu.SMEM((32,), F32),
            pltpu.SMEM((1,), F32),
            pltpu.VMEM((3, NG), jnp.int32),
            pltpu.VMEM((16, GRID), BF16),
            pltpu.SemaphoreType.DMA((7,)),
        ],
        mib=60,
        cost=pl.CostEstimate(flops=1 << 26, bytes_accessed=1 << 20, transcendentals=0),
    )(
        ids,
        valence_select,
        shifted_index,
        valence_energy,
        conduction_energy.reshape(32),
        frequency,
        wave_vectors,
        xtab,
    )
    partial = call(
        density_kernel,
        "density",
        ((8, 8, 1024), BF16),
        [SM, HB] + [VM] * 6,
        [
            pltpu.VMEM((NOCC, GRID, SLAB, 128), BF16),
            pltpu.VMEM((512, 128), BF16),
            pltpu.VMEM((512, 128), BF16),
            pltpu.VMEM((2, 512, 256), BF16),
            pltpu.VMEM((1024, 1024), BF16),
            pltpu.VMEM((256, 1024), BF16),
            pltpu.SemaphoreType.DMA((NOCC,)),
        ],
        mib=61,
    )(valence_select, valence_orbitals, phase, cond, wave_vectors, ymat, zmat, pick)
    recv = lax.all_to_all(partial, BAND, split_axis=0, concat_axis=0, tiled=True)
    packed = call(pack_kernel, "pack", ((64, 16, 128), BF16), [VM, VM])(weight, recv)
    recv = lax.all_to_all(packed, ("z",) + BAND, split_axis=0, concat_axis=0, tiled=True)
    chi = call(
        chi_kernel, "chi", ((32, 16, 256), BF16), [VM], [pltpu.VMEM((1024, 128), F32)]
    )(recv)
    recv = lax.all_to_all(chi, ("xh", "c") + BAND, split_axis=0, concat_axis=0, tiled=True)
    return call(final_kernel, "final", ((2, 8, NG), F32), [VM])(recv)


def solution(mesh):
    fine = Mesh(mesh.devices.reshape(2, 8, 2, 2, 4), AXES)
    in_specs = (
        P(KA, None, None, BAND, None),
        P(None, None, KA, BAND, None),
        P(KA, None),
        P(),
        P(KA, None),
        P(),
        P(),
        P(),
    )
    out_specs = P(None, AXES, None)
    return jax.shard_map(shards, mesh=fine, in_specs=in_specs, out_specs=out_specs, check_vma=False)
```

time: 86.6 us -> 76.7 us (0.89)
  blocking collectives: 33.5 us -> 41.1 us
  waiting for transfers between devices: 12.7 us -> 6.87 us
  starting transfers between devices: 16.8 us -> 12.6 us
  local copies, waits for them, and re-layouts: 5.29 us -> 1.3 us
  Pallas kernels: 16.3 us -> 13.1 us
    all_to_all x0 -> x1, blocking collectives: none -> 9.66 us  [shards(): lax.all_to_all(partial, BAND, split_axis=0, concat_axis=0, tiled=True)]
    all_to_all x1 -> x0, starting transfers between devices: 4.24 us -> none  [shards(): lax.all_to_all(partial, BAND, split_axis=0, concat_axis=0, tiled=True)]
    all_to_all x1 -> x0, waiting for transfers between devices: 3.5 us -> none  [shards(): lax.all_to_all(partial, BAND, split_axis=0, concat_axis=0, tiled=True)]
    pallas_call x4 -> x6, Pallas kernels: 16.3 us -> 13.1 us  [the longest x1 8.69 us: shards(): call(density_kernel, 'density', ((8, 8, 1024), BF16), [SM, HB] + [VM] * 6...]
    all_to_all x1, waiting for transfers between devices: 9.2 us -> 6.87 us  [shards(): cond = lax.all_to_all(ordered, KA, split_axis=0, concat_axis=0, tiled=True)]
    squeeze x1 -> x0, local copies, waits for them, and re-layouts: 1.29 us -> none  [shards(): xown = lax.dynamic_index_in_dim(jnp.asarray(xtab), band, 0, keepdims=False)]
    gather x1 -> x0, local copies, waits for them, and re-layouts: 1.24 us -> none  [shards(): conduction_orbitals[:, 0].at[shifted_index].get(mode='promise_in_bounds')]
    all_to_all x1, blocking collectives: 17.5 us -> 16.3 us  [shards(): lax.all_to_all(chi, ('xh', 'c') + BAND, split_axis=0, concat_axis=0, tile...]
  transfers between devices with their start and end apart: 2 -> 1, of which waited for: 2 -> 1; matrix products, arithmetic and copies ran while one was open for 3% -> 1% of each run, Pallas kernels for 0% -> 2%
where the time goes in v2:
time: 76.7 us; the launch traced here: 76.2 us
  blocking collectives  41.1 us (54%)
  Pallas kernels  13.1 us (17%)
  starting transfers between devices  12.6 us (16%)
  waiting for transfers between devices  6.87 us (9%)
  local copies, waits for them, and re-layouts  1.3 us (2%)
    all_to_all x1, blocking collectives, shards(): lax.all_to_all(chi, ('xh', 'c') + BAND, split_axis=0, concat_axis=0, tile...  16.3 us
    all_to_all x1, blocking collectives, shards(): lax.all_to_all(packed, ('z',) + BAND, split_axis=0, concat_axis=0, tiled=...  15.1 us
    all_to_all x1, starting transfers between devices, shards(): cond = lax.all_to_all(ordered, KA, split_axis=0, concat_axis=0, tiled=True)  12.6 us
    all_to_all x1, blocking collectives, shards(): lax.all_to_all(partial, BAND, split_axis=0, concat_axis=0, tiled=True)  9.66 us
    pallas_call x1, Pallas kernels, shards(): call(density_kernel, 'density', ((8, 8, 1024), BF16), [SM, HB] + [VM] * 6...  8.69 us
    all_to_all x1, waiting for transfers between devices, shards(): cond = lax.all_to_all(ordered, KA, split_axis=0, concat_axis=0, tiled=True)  6.87 us
    pallas_call x1, Pallas kernels, shards(): call(prep_kernel, 'prep', [((16, NG), F32), ((8, 128), F32)], [SM] + [HB]...  1.71 us
    pallas_call x1, Pallas kernels, shards(): call(order_kernel, 'order', ((32, 2, SLAB, 128), BF16), [HB, HB], [pltpu....  1.59 us
  transfers between devices with their start and end apart: 1, of which 1 were waited for; matrix products, arithmetic and copies ran while one was open for 1% of the time, Pallas kernels for 2%

profile of v2, /device:TPU:1, one launch (start us, length us, event | category | flops | bytes accessed | tf_op | source)
XLA Modules:
  0.0 76.2 jit_solution(10373352869237311925)
XLA Ops:
  0.0 1.6 %order.1 = bf16[32,2,8,128]{3,2,1,0:T(8,128)(2,1)} custom-call(s32[32]{0:T(128)} %shift.1, bf16[32,1,2,8,128]{4,3,2,1,0:T(8,128)(2,1)} %cond.1), custom_call_target="tpu_custom_call" | custom-call | tf_op jit(solution)/shard_map/order/pallas_call | solution.py:235
  1.6 12.6 %all-to-all-start = ((bf16[32,2,8,128]{3,2,1,0:T(8,128)(2,1)}), bf16[32,2,8,128]{3,2,1,0:T(8,128)(2,1)S(1)}, u32[]{:S(2)}, u32[]{:S(2)}) async-start(bf16[32,2,8,128]{3,2,1,0:T(8,128)(2,1)} %order.1), calls=%async_computation | async-start | bytes 262144 | tf_op jit(solution)/shard_map/all_to_all | solution.py:247
  14.8 0.6 pad_add_fusion.ids
  15.4 1.7 %prep.1 = (f32[16,2048]{1,0:T(8,128)S(1)}, f32[8,128]{1,0:T(8,128)S(1)}) custom-call(s32[2]{0:T(128)} %pad_add_fusion.ids, s32[1,16]{1,0:T(1,128)} %sel.1, s32[32]{0:T(128)} %shift.1, f32[1,32]{1,0:T(1,128)} %vale_h.1, f32[32]{0:T(128)} %bitcast.3, f32[1]{0:T(128)S(6)} %copy.13.freq_h, s32[3,2048]{1,0:T(4,128)} %waves.1, ...), custom_call_target="tpu_custom_call" | custom-call | flops 67108864 | bytes 1048576 | tf_op jit(solution)/shard_map/prep/pallas_call | solution.py:248
  17.2 0.0 copy-start
  17.2 0.6 copy-done
  17.8 6.9 %all-to-all-done.cond = bf16[32,2,8,128]{3,2,1,0:T(8,128)(2,1)S(1)} async-done(((bf16[32,2,8,128]{3,2,1,0:T(8,128)(2,1)}), bf16[32,2,8,128]{3,2,1,0:T(8,128)(2,1)S(1)}, u32[]{:S(2)}, u32[]{:S(2)}) %all-to-all-start) | async-done | bytes 131104 | tf_op jit(solution)/shard_map/all_to_all | solution.py:247
  24.7 0.0 copy-start.1
  24.7 0.7 copy-done.1
  25.3 8.7 %density.1 = bf16[8,8,1024]{2,1,0:T(8,128)(2,1)} custom-call(s32[1,16]{1,0:T(1,128)} %sel.1, bf16[1,32,64,8,128]{4,3,2,1,0:T(8,128)(2,1)} %val.1, f32[16,2048]{1,0:T(8,128)} %copy-done, bf16[32,2,8,128]{3,2,1,0:T(8,128)(2,1)} %copy-done.1, s32[3,2048]{1,0:T(4,128)} %waves.1, bf16[512,512]{1,0:T(8,128)(2,1)} %constant.35.clone.ymat, ...), custom_call_target="tpu_custom_call" | custom-call | tf_op jit(solution)/shard_map/density/pallas_call | solution.py:275
  34.0 9.7 %all_to_all.20.recv = bf16[8,8,1024]{2,1,0:T(8,128)(2,1)S(1)} all-to-all(bf16[8,8,1024]{2,1,0:T(8,128)(2,1)} %density.1), channel_id=1, replica_groups=mesh['xh'=2,'z'=8,'c'=2,'xl'=2,'y'=4] {'xl','y'}, dimensions={0} | all-to-all | bytes 262144 | tf_op jit(solution)/shard_map/all_to_all | solution.py:291
  43.7 15.1 %all_to_all.21.recv = bf16[64,16,128]{2,1,0:T(8,128)(2,1)S(1)} all-to-all(bf16[64,16,128]{2,1,0:T(8,128)(2,1)S(1)} %pack.1), channel_id=1, replica_groups=mesh['xh'=2,'z'=8,'c'=2,'xl'=2,'y'=4] {'z','xl','y'}, dimensions={0} | all-to-all | bytes 524288 | tf_op jit(solution)/shard_map/all_to_all | solution.py:293
  58.9 0.4 chi.1
  59.3 16.3 %all_to_all.22.recv = bf16[32,16,256]{2,1,0:T(8,128)(2,1)S(1)} all-to-all(bf16[32,16,256]{2,1,0:T(8,128)(2,1)S(1)} %chi.1), channel_id=1, replica_groups=mesh['xh'=2,'z'=8,'c'=2,'xl'=2,'y'=4] {'xh','c','xl','y'}, dimensions={0} | all-to-all | bytes 524288 | tf_op jit(solution)/shard_map/all_to_all | solution.py:297
  75.5 0.7 final.1
  (1 shorter events, 0.0 us)
Async XLA Ops:
  1.6 23.1 %all-to-all-start = ((bf16[32,2,8,128]{3,2,1,0:T(8,128)(2,1)}), bf16[32,2,8,128]{3,2,1,0:T(8,128)(2,1)S(1)}, u32[]{:S(2)}, u32[]{:S(2)}) async-start(bf16[32,2,8,128]{3,2,1,0:T(8,128)(2,1)} %order.1), calls=%async_computation | async-start | bytes 262144 | tf_op jit(solution)/shard_map/all_to_all | solution.py:247
  17.2 0.7 copy-start
  24.7 0.7 copy-start.1

commit v3 on v2

--- a/solution.py
+++ b/solution.py
@@ -62,8 +62,8 @@
         out[k] = rows[idx[k], 0]
 
 
-def prep_kernel(ids, sel_h, shift_h, vale_h, conde_h, freq_h, waves_h, xtab_h, phase, weight,
-                sel, shift, val_e, cond_e, freq, waves, xtab, sems):
+def prep_kernel(ids, sel_h, shift_h, vale_h, conde_h, freq_h, waves_h, xtab_h, val, ymat_h, zmat_h, phase, weight, vbuf, ymat, zmat,
+                sel, shift, val_e, cond_e, freq, waves, xtab, sems, vsems):
     pairs = [
         (sel_h, sel),
         (xtab_h.at[ids[1]], xtab),
@@ -72,11 +72,20 @@
         (vale_h, val_e),
         (conde_h, cond_e),
         (freq_h, freq),
+        (ymat_h, ymat),
+        (zmat_h, zmat),
     ]
     copies = [pltpu.make_async_copy(a, b, sems.at[i]) for i, (a, b) in enumerate(pairs)]
     for copy in copies:
         copy.start()
-    for copy in copies:
+    copies[0].wait()
+    fetch = [
+        pltpu.make_async_copy(val.at[0, sel[0, j]], vbuf.at[j], vsems.at[j])
+        for j in range(NOCC)
+    ]
+    for copy in fetch:
+        copy.start()
+    for copy in copies[1:]:
         copy.wait()
     gx = waves[0:1, :] + HALF // 2
     hot = (lax.broadcasted_iota(jnp.int32, (2 * HALF, NG), 0) % HALF == gx)
@@ -89,22 +98,16 @@
     gap = jnp.where((rows // 2) % 2 == 0, d0, d1)
     w = freq[0]
     weight[...] = 2.0 * gap / (gap * gap + w * w) / 512.0
-
-
-def density_kernel(sel, val, phase, cond, waves, ymat, zmat, pick, out, vbuf, c1, c2, pbuf, gbuf, fbuf, sems):
-    copies = [
-        pltpu.make_async_copy(val.at[0, sel[0, j]], vbuf.at[j], sems.at[j])
-        for j in range(NOCC)
-    ]
-    for copy in copies:
-        copy.start()
+    for copy in fetch:
+        copy.wait()
+
+
+def density_kernel(vbuf, phase, cond, waves, ymat, zmat, pick, out, c1, c2, pbuf, gbuf, fbuf):
     low = lax.broadcasted_iota(jnp.int32, (512, 128), 1) < GRID
     cf = cond[...].reshape(512, 128).astype(jnp.float32)
     cr = pltpu.roll(cf, GRID, 1)
     c1[...] = jnp.where(low, cf, cr).astype(jnp.bfloat16)
     c2[...] = jnp.where(low, cr, -cf).astype(jnp.bfloat16)
-    for copy in copies:
-        copy.wait()
 
     for p in range(NOCC // 2):
         for q in range(2):
@@ -121,10 +124,14 @@
                 lane = ((gy % 4) * 2 + w) * 128
                 gbuf[row:row + 16, lane:lane + 128] = g[w, gy]
 
-    f = jnp.dot(gbuf[...], zmat[...], preferred_element_type=jnp.float32).astype(jnp.bfloat16)
-    for k in range(8):
-        fbuf[0:128, 128 * k:128 * (k + 1)] = f[128 * k:128 * (k + 1), :128]
-        fbuf[128:256, 128 * k:128 * (k + 1)] = f[128 * k:128 * (k + 1), 128:]
+    for n in range(2):
+        f = jnp.dot(
+            gbuf[512 * n:512 * (n + 1), :], zmat[...], preferred_element_type=jnp.float32
+        ).astype(jnp.bfloat16)
+        for k in range(4):
+            lane = (4 * n + k) * 128
+            fbuf[0:128, lane:lane + 128] = f[128 * k:128 * (k + 1), :128]
+            fbuf[128:256, lane:lane + 128] = f[128 * k:128 * (k + 1), 128:]
 
     for n in range(4):
         parts = []
@@ -245,11 +252,11 @@
         mib=63,
     )(shifted_index, conduction_orbitals)
     cond = lax.all_to_all(ordered, KA, split_axis=0, concat_axis=0, tiled=True)
-    phase, weight = call(
+    phase, weight, vbuf, ymat, zmat = call(
         prep_kernel,
         "prep",
-        [((16, NG), F32), ((8, 128), F32)],
-        [SM] + [HB] * 7,
+        [((16, NG), F32), ((8, 128), F32), ((NOCC, GRID, SLAB, 128), BF16), ((512, 512), BF16), ((1024, 256), BF16)],
+        [SM] + [HB] * 10,
         [
             pltpu.SMEM((1, NOCC), jnp.int32),
             pltpu.SMEM((32,), jnp.int32),
@@ -258,9 +265,10 @@
             pltpu.SMEM((1,), F32),
             pltpu.VMEM((3, NG), jnp.int32),
             pltpu.VMEM((16, GRID), BF16),
-            pltpu.SemaphoreType.DMA((7,)),
+            pltpu.SemaphoreType.DMA((9,)),
+            pltpu.SemaphoreType.DMA((NOCC,)),
         ],
-        mib=60,
+        mib=57,
         cost=pl.CostEstimate(flops=1 << 26, bytes_accessed=1 << 20, transcendentals=0),
     )(
         ids,
@@ -271,23 +279,24 @@
         frequency,
         wave_vectors,
         xtab,
+        valence_orbitals,
+        ymat,
+        zmat,
     )
     partial = call(
         density_kernel,
         "density",
         ((8, 8, 1024), BF16),
-        [SM, HB] + [VM] * 6,
+        [VM] * 7,
         [
-            pltpu.VMEM((NOCC, GRID, SLAB, 128), BF16),
             pltpu.VMEM((512, 128), BF16),
             pltpu.VMEM((512, 128), BF16),
             pltpu.VMEM((2, 512, 256), BF16),
             pltpu.VMEM((1024, 1024), BF16),
             pltpu.VMEM((256, 1024), BF16),
-            pltpu.SemaphoreType.DMA((NOCC,)),
         ],
-        mib=61,
-    )(valence_select, valence_orbitals, phase, cond, wave_vectors, ymat, zmat, pick)
+        mib=8,
+    )(vbuf, phase, cond, wave_vectors, ymat, zmat, pick)
     recv = lax.all_to_all(partial, BAND, split_axis=0, concat_axis=0, tiled=True)
     packed = call(pack_kernel, "pack", ((64, 16, 128), BF16), [VM, VM])(weight, recv)
     recv = lax.all_to_all(packed, ("z",) + BAND, split_axis=0, concat_axis=0, tiled=True)

time: 76.7 us -> 71.5 us (0.932)
  Pallas kernels: 13.1 us -> 10.1 us
  local copies, waits for them, and re-layouts: 1.3 us -> 0.01 us
  waiting for transfers between devices: 6.87 us -> 6.04 us
    pallas_call x2, Pallas kernels: 10.4 us -> 7.42 us  [the longest x1 4.3 us: shards(): call(density_kernel, 'density', ((8, 8, 1024), BF16), [VM] * 7, [pltpu.VM...]
    unnamed x4, local copies, waits for them, and re-layouts: 1.3 us -> 0.01 us
    all_to_all x1, waiting for transfers between devices: 6.87 us -> 6.04 us  [shards(): cond = lax.all_to_all(ordered, KA, split_axis=0, concat_axis=0, tiled=True)]
  transfers between devices with their start and end apart: 1 -> 1, of which waited for: 1 -> 1; matrix products, arithmetic and copies ran while one was open for 1% -> 1% of each run, Pallas kernels for 2% -> 4%
where the time goes in v3:
time: 71.5 us; the launch traced here: 71.2 us
  blocking collectives  41 us (57%)
  starting transfers between devices  12.6 us (18%)
  Pallas kernels  10.1 us (14%)
  waiting for transfers between devices  6.04 us (8%)
    all_to_all x1, blocking collectives, shards(): lax.all_to_all(chi, ('xh', 'c') + BAND, split_axis=0, concat_axis=0, tile...  16.5 us
    all_to_all x1, blocking collectives, shards(): lax.all_to_all(packed, ('z',) + BAND, split_axis=0, concat_axis=0, tiled=...  15.1 us
    all_to_all x1, starting transfers between devices, shards(): cond = lax.all_to_all(ordered, KA, split_axis=0, concat_axis=0, tiled=True)  12.6 us
    all_to_all x1, blocking collectives, shards(): lax.all_to_all(partial, BAND, split_axis=0, concat_axis=0, tiled=True)  9.45 us
    all_to_all x1, waiting for transfers between devices, shards(): cond = lax.all_to_all(ordered, KA, split_axis=0, concat_axis=0, tiled=True)  6.04 us
    pallas_call x1, Pallas kernels, shards(): call(density_kernel, 'density', ((8, 8, 1024), BF16), [VM] * 7, [pltpu.VM...  4.3 us
    pallas_call x1, Pallas kernels, shards(): call(prep_kernel, 'prep', [((16, NG), F32), ((8, 128), F32), ((NOCC, GRID...  3.12 us
    pallas_call x1, Pallas kernels, shards(): call(order_kernel, 'order', ((32, 2, SLAB, 128), BF16), [HB, HB], [pltpu....  1.63 us
  transfers between devices with their start and end apart: 1, of which 1 were waited for; matrix products, arithmetic and copies ran while one was open for 1% of the time, Pallas kernels for 4%

profile of v3, /device:TPU:1, one launch (start us, length us, event | category | flops | bytes accessed | tf_op | source)
XLA Modules:
  0.0 71.2 jit_solution(2877038585523526488)
XLA Ops:
  0.0 0.0 copy-start.1
  0.0 0.0 copy-start
  0.0 1.6 %order.1 = bf16[32,2,8,128]{3,2,1,0:T(8,128)(2,1)} custom-call(s32[32]{0:T(128)} %shift.1, bf16[32,1,2,8,128]{4,3,2,1,0:T(8,128)(2,1)} %cond.1), custom_call_target="tpu_custom_call" | custom-call | tf_op jit(solution)/shard_map/order/pallas_call | solution.py:242
  1.6 12.6 %all-to-all-start = ((bf16[32,2,8,128]{3,2,1,0:T(8,128)(2,1)}), bf16[32,2,8,128]{3,2,1,0:T(8,128)(2,1)S(1)}, u32[]{:S(2)}, u32[]{:S(2)}) async-start(bf16[32,2,8,128]{3,2,1,0:T(8,128)(2,1)} %order.1), calls=%async_computation | async-start | bytes 262144 | tf_op jit(solution)/shard_map/all_to_all | solution.py:254
  14.9 0.7 pad_add_fusion.ids
  15.6 3.1 %prep.1 = (f32[16,2048]{1,0:T(8,128)S(1)}, f32[8,128]{1,0:T(8,128)S(1)}, bf16[16,64,8,128]{3,2,1,0:T(8,128)(2,1)S(1)}, bf16[512,512]{1,0:T(8,128)(2,1)S(1)}, bf16[1024,256]{1,0:T(8,128)(2,1)S(1)}) custom-call(s32[2]{0:T(128)} %pad_add_fusion.ids, s32[1,16]{1,0:T(1,128)} %sel_h.1, s32[32]{0:T(128)} %shift.1, f32[1,32]{1,0:T(1,128)} %vale_h.1, f32[32]{0:T(128)} %bitcast.3, ...), custom_call_target="tpu_custom_call" | custom-call | flops 67108864 | bytes 1048576 | tf_op jit(solution)/shard_map/prep/pallas_call | solution.py:255
  18.7 6.0 %all-to-all-done.cond = bf16[32,2,8,128]{3,2,1,0:T(8,128)(2,1)S(1)} async-done(((bf16[32,2,8,128]{3,2,1,0:T(8,128)(2,1)}), bf16[32,2,8,128]{3,2,1,0:T(8,128)(2,1)S(1)}, u32[]{:S(2)}, u32[]{:S(2)}) %all-to-all-start) | async-done | bytes 131104 | tf_op jit(solution)/shard_map/all_to_all | solution.py:254
  24.7 0.0 copy-done.1
  24.7 0.0 copy-done
  24.7 4.3 %density.1 = bf16[8,8,1024]{2,1,0:T(8,128)(2,1)S(1)} custom-call(bf16[16,64,8,128]{3,2,1,0:T(8,128)(2,1)S(1)} %get-tuple-element.11.vbuf, f32[16,2048]{1,0:T(8,128)S(1)} %get-tuple-element.12.phase, bf16[32,2,8,128]{3,2,1,0:T(8,128)(2,1)S(1)} %all-to-all-done.cond, s32[3,2048]{1,0:T(4,128)S(1)} %copy-done, bf16[512,512]{1,0:T(8,128)(2,1)S(1)} %get-tuple-element.13.ymat, ...), custom_call_target="tpu_custom_call" | custom-call | tf_op jit(solution)/shard_map/density/pallas_call | solution.py:286
  29.0 9.4 %all_to_all.20.recv = bf16[8,8,1024]{2,1,0:T(8,128)(2,1)S(1)} all-to-all(bf16[8,8,1024]{2,1,0:T(8,128)(2,1)S(1)} %density.1), channel_id=1, replica_groups=mesh['xh'=2,'z'=8,'c'=2,'xl'=2,'y'=4] {'xl','y'}, dimensions={0} | all-to-all | bytes 262144 | tf_op jit(solution)/shard_map/all_to_all | solution.py:300
  38.5 15.1 %all_to_all.21.recv = bf16[64,16,128]{2,1,0:T(8,128)(2,1)S(1)} all-to-all(bf16[64,16,128]{2,1,0:T(8,128)(2,1)S(1)} %pack.1), channel_id=1, replica_groups=mesh['xh'=2,'z'=8,'c'=2,'xl'=2,'y'=4] {'z','xl','y'}, dimensions={0} | all-to-all | bytes 524288 | tf_op jit(solution)/shard_map/all_to_all | solution.py:302
  53.7 0.4 chi.1
  54.0 16.5 %all_to_all.22.recv = bf16[32,16,256]{2,1,0:T(8,128)(2,1)S(1)} all-to-all(bf16[32,16,256]{2,1,0:T(8,128)(2,1)S(1)} %chi.1), channel_id=1, replica_groups=mesh['xh'=2,'z'=8,'c'=2,'xl'=2,'y'=4] {'xh','c','xl','y'}, dimensions={0} | all-to-all | bytes 524288 | tf_op jit(solution)/shard_map/all_to_all | solution.py:306
  70.5 0.7 final.1
  (1 shorter events, 0.0 us)
Async XLA Ops:
  0.0 24.7 %copy-start.1 = (bf16[64,512]{1,0:T(8,128)(2,1)S(1)}, bf16[64,512]{1,0:T(8,128)(2,1)}, u32[]{:S(2)}) copy-start(bf16[64,512]{1,0:T(8,128)(2,1)} %constant.37.clone.pick) | copy-start | bytes 196612
  0.0 24.7 %copy-start = (s32[3,2048]{1,0:T(4,128)S(1)}, s32[3,2048]{1,0:T(4,128)}, u32[]{:S(2)}) copy-start(s32[3,2048]{1,0:T(4,128)} %waves.1) | copy-start | bytes 73732
  1.6 23.1 %all-to-all-start = ((bf16[32,2,8,128]{3,2,1,0:T(8,128)(2,1)}), bf16[32,2,8,128]{3,2,1,0:T(8,128)(2,1)S(1)}, u32[]{:S(2)}, u32[]{:S(2)}) async-start(bf16[32,2,8,128]{3,2,1,0:T(8,128)(2,1)} %order.1), calls=%async_computation | async-start | bytes 262144 | tf_op jit(solution)/shard_map/all_to_all | solution.py:254

commit v4 on v3

--- a/solution.py
+++ b/solution.py
@@ -164,7 +164,8 @@
             ).astype(jnp.bfloat16)
 
 
-def chi_kernel(recv, out, buf):
+def chi_kernel(recv, own, send, buf):
+    upper = lax.axis_index("c") == 1
     buf[...] = recv[...].astype(jnp.float32).reshape(1024, 128)
 
     def rows(kind, h, j, c):
@@ -189,14 +190,18 @@
         chi = jnp.concatenate(
             [chi[:128].reshape(16, 8, 256), chi[128:].reshape(16, 8, 256)], axis=1
         )
-        out[16 * h:16 * (h + 1)] = chi.astype(jnp.bfloat16)
+        low, high = chi[:8], chi[8:]
+        own[8 * h:8 * (h + 1)] = jnp.where(upper, high, low).astype(jnp.bfloat16)
+        send[8 * h:8 * (h + 1)] = jnp.where(upper, low, high).astype(jnp.bfloat16)
+
+
+def merge_kernel(own, other, out):
+    out[...] = (own[...].astype(jnp.float32) + other[...].astype(jnp.float32)).astype(jnp.bfloat16)
 
 
 def final_kernel(recv, out):
     for b in range(8):
-        acc = recv[b].astype(jnp.float32)
-        for s in range(1, 4):
-            acc = acc + recv[8 * s + b].astype(jnp.float32)
+        acc = recv[b].astype(jnp.float32) + recv[8 + b].astype(jnp.float32)
         for h in range(2):
             lane = h * 1024 + b * 128
             out[0, :, lane:lane + 128] = acc[:8, 128 * h:128 * (h + 1)]
@@ -300,10 +305,16 @@
     recv = lax.all_to_all(partial, BAND, split_axis=0, concat_axis=0, tiled=True)
     packed = call(pack_kernel, "pack", ((64, 16, 128), BF16), [VM, VM])(weight, recv)
     recv = lax.all_to_all(packed, ("z",) + BAND, split_axis=0, concat_axis=0, tiled=True)
-    chi = call(
-        chi_kernel, "chi", ((32, 16, 256), BF16), [VM], [pltpu.VMEM((1024, 128), F32)]
+    own, send = call(
+        chi_kernel,
+        "chi",
+        [((16, 16, 256), BF16)] * 2,
+        [VM],
+        [pltpu.VMEM((1024, 128), F32)],
     )(recv)
-    recv = lax.all_to_all(chi, ("xh", "c") + BAND, split_axis=0, concat_axis=0, tiled=True)
+    other = lax.ppermute(send, "c", [(0, 1), (1, 0)])
+    merged = call(merge_kernel, "merge", ((16, 16, 256), BF16), [VM, VM])(own, other)
+    recv = lax.all_to_all(merged, ("xh",) + BAND, split_axis=0, concat_axis=0, tiled=True)
     return call(final_kernel, "final", ((2, 8, NG), F32), [VM])(recv)
 
 

time: 71.5 us -> 70 us (0.979)
  blocking collectives: 41 us -> 34.6 us
  starting transfers between devices: 12.6 us -> 16.5 us
  waiting for transfers between devices: 6.04 us -> 7.04 us
    all_to_all x1, blocking collectives: 16.5 us -> 10.1 us  [shards(): lax.all_to_all(merged, ('xh',) + BAND, split_axis=0, concat_axis=0, tiled...]
    ppermute x0 -> x1, starting transfers between devices: none -> 3.92 us  [shards(): other = lax.ppermute(send, 'c', [(0, 1), (1, 0)])]
    ppermute x0 -> x1, waiting for transfers between devices: none -> 0.99 us  [shards(): other = lax.ppermute(send, 'c', [(0, 1), (1, 0)])]
  transfers between devices with their start and end apart: 1 -> 2, of which waited for: 1 -> 2; matrix products, arithmetic and copies ran while one was open for 1% -> 1% of each run, Pallas kernels for 4% -> 4%
where the time goes in v4:
time: 70 us; the launch traced here: 69.7 us
  blocking collectives  34.6 us (49%)
  starting transfers between devices  16.5 us (24%)
  Pallas kernels  10.2 us (15%)
  waiting for transfers between devices  7.04 us (10%)
  between operations  0.71 us (1%)
    all_to_all x1, blocking collectives, shards(): lax.all_to_all(packed, ('z',) + BAND, split_axis=0, concat_axis=0, tiled=...  15.1 us
    all_to_all x1, starting transfers between devices, shards(): cond = lax.all_to_all(ordered, KA, split_axis=0, concat_axis=0, tiled=True)  12.6 us
    all_to_all x1, blocking collectives, shards(): lax.all_to_all(merged, ('xh',) + BAND, split_axis=0, concat_axis=0, tiled...  10.1 us
    all_to_all x1, blocking collectives, shards(): lax.all_to_all(partial, BAND, split_axis=0, concat_axis=0, tiled=True)  9.45 us
    all_to_all x1, waiting for transfers between devices, shards(): cond = lax.all_to_all(ordered, KA, split_axis=0, concat_axis=0, tiled=True)  6.06 us
    pallas_call x1, Pallas kernels, shards(): call(density_kernel, 'density', ((8, 8, 1024), BF16), [VM] * 7, [pltpu.VM...  4.3 us
    ppermute x1, starting transfers between devices, shards(): other = lax.ppermute(send, 'c', [(0, 1), (1, 0)])  3.92 us
    pallas_call x1, Pallas kernels, shards(): call(prep_kernel, 'prep', [((16, NG), F32), ((8, 128), F32), ((NOCC, GRID...  3.12 us
  transfers between devices with their start and end apart: 2, of which 2 were waited for; matrix products, arithmetic and copies ran while one was open for 1% of the time, Pallas kernels for 4%

profile of v4, /device:TPU:1, one launch (start us, length us, event | category | flops | bytes accessed | tf_op | source)
XLA Modules:
  0.0 69.7 jit_solution(13321192281464130119)
XLA Ops:
  0.0 0.0 copy-start.1
  0.0 0.0 copy-start
  0.0 1.6 %order.1 = bf16[32,2,8,128]{3,2,1,0:T(8,128)(2,1)} custom-call(s32[32]{0:T(128)} %shift.1, bf16[32,1,2,8,128]{4,3,2,1,0:T(8,128)(2,1)} %cond.1), custom_call_target="tpu_custom_call" | custom-call | tf_op jit(solution)/shard_map/order/pallas_call | solution.py:247
  1.6 12.6 %all-to-all-start = ((bf16[32,2,8,128]{3,2,1,0:T(8,128)(2,1)}), bf16[32,2,8,128]{3,2,1,0:T(8,128)(2,1)S(1)}, u32[]{:S(2)}, u32[]{:S(2)}) async-start(bf16[32,2,8,128]{3,2,1,0:T(8,128)(2,1)} %order.1), calls=%async_computation | async-start | bytes 262144 | tf_op jit(solution)/shard_map/all_to_all | solution.py:259
  14.9 0.7 pad_add_fusion.ids
  15.5 3.1 %prep.1 = (f32[16,2048]{1,0:T(8,128)S(1)}, f32[8,128]{1,0:T(8,128)S(1)}, bf16[16,64,8,128]{3,2,1,0:T(8,128)(2,1)S(1)}, bf16[512,512]{1,0:T(8,128)(2,1)S(1)}, bf16[1024,256]{1,0:T(8,128)(2,1)S(1)}) custom-call(s32[2]{0:T(128)} %pad_add_fusion.ids, s32[1,16]{1,0:T(1,128)} %sel_h.1, s32[32]{0:T(128)} %shift.1, f32[1,32]{1,0:T(1,128)} %vale_h.1, f32[32]{0:T(128)} %bitcast.3, ...), custom_call_target="tpu_custom_call" | custom-call | flops 67108864 | bytes 1048576 | tf_op jit(solution)/shard_map/prep/pallas_call | solution.py:260
  18.7 6.1 %all-to-all-done.cond = bf16[32,2,8,128]{3,2,1,0:T(8,128)(2,1)S(1)} async-done(((bf16[32,2,8,128]{3,2,1,0:T(8,128)(2,1)}), bf16[32,2,8,128]{3,2,1,0:T(8,128)(2,1)S(1)}, u32[]{:S(2)}, u32[]{:S(2)}) %all-to-all-start) | async-done | bytes 131104 | tf_op jit(solution)/shard_map/all_to_all | solution.py:259
  24.7 0.0 copy-done.1
  24.7 0.0 copy-done
  24.7 4.3 %density.1 = bf16[8,8,1024]{2,1,0:T(8,128)(2,1)S(1)} custom-call(bf16[16,64,8,128]{3,2,1,0:T(8,128)(2,1)S(1)} %get-tuple-element.13.vbuf, f32[16,2048]{1,0:T(8,128)S(1)} %get-tuple-element.14.phase, bf16[32,2,8,128]{3,2,1,0:T(8,128)(2,1)S(1)} %all-to-all-done.cond, s32[3,2048]{1,0:T(4,128)S(1)} %copy-done, bf16[512,512]{1,0:T(8,128)(2,1)S(1)} %get-tuple-element.15.ymat, ...), custom_call_target="tpu_custom_call" | custom-call | tf_op jit(solution)/shard_map/density/pallas_call | solution.py:291
  29.0 9.4 %all_to_all.20.recv = bf16[8,8,1024]{2,1,0:T(8,128)(2,1)S(1)} all-to-all(bf16[8,8,1024]{2,1,0:T(8,128)(2,1)S(1)} %density.1), channel_id=1, replica_groups=mesh['xh'=2,'z'=8,'c'=2,'xl'=2,'y'=4] {'xl','y'}, dimensions={0} | all-to-all | bytes 262144 | tf_op jit(solution)/shard_map/all_to_all | solution.py:305
  38.5 15.1 %all_to_all.21.recv = bf16[64,16,128]{2,1,0:T(8,128)(2,1)S(1)} all-to-all(bf16[64,16,128]{2,1,0:T(8,128)(2,1)S(1)} %pack.1), channel_id=1, replica_groups=mesh['xh'=2,'z'=8,'c'=2,'xl'=2,'y'=4] {'z','xl','y'}, dimensions={0} | all-to-all | bytes 524288 | tf_op jit(solution)/shard_map/all_to_all | solution.py:307
  53.7 0.4 chi.1
  54.0 3.9 %collective-permute-start = (bf16[16,16,256]{2,1,0:T(8,128)(2,1)S(1)}, bf16[16,16,256]{2,1,0:T(8,128)(2,1)S(1)}, u32[]{:S(2)}, u32[]{:S(2)}) collective-permute-start(bf16[16,16,256]{2,1,0:T(8,128)(2,1)S(1)} %get-tuple-element.18), channel_id=1, source_target_pairs={{0,8},{8,0},{1,9},{9,1},{2,10},{10,2},{3,11},{11,3},{4,12},{12,4},... | collective-permute-start | bytes 393224 | tf_op jit(solution)/shard_map/ppermute | solution.py:315
  58.0 1.0 %collective-permute-done.other = bf16[16,16,256]{2,1,0:T(8,128)(2,1)S(1)} collective-permute-done((bf16[16,16,256]{2,1,0:T(8,128)(2,1)S(1)}, bf16[16,16,256]{2,1,0:T(8,128)(2,1)S(1)}, u32[]{:S(2)}, u32[]{:S(2)}) %collective-permute-start) | collective-permute-done | bytes 131104 | tf_op jit(solution)/shard_map/ppermute | solution.py:315
  59.0 10.1 %all_to_all.22.recv = bf16[16,16,256]{2,1,0:T(8,128)(2,1)S(1)} all-to-all(bf16[16,16,256]{2,1,0:T(8,128)(2,1)S(1)} %merge.1), channel_id=1, replica_groups=mesh['xh'=2,'z'=8,'c'=2,'xl'=2,'y'=4] {'xh','xl','y'}, dimensions={0} | all-to-all | bytes 262144 | tf_op jit(solution)/shard_map/all_to_all | solution.py:317
  69.1 0.7 final.1
  (2 shorter events, 0.1 us)
Async XLA Ops:
  0.0 24.7 %copy-start.1 = (bf16[64,512]{1,0:T(8,128)(2,1)S(1)}, bf16[64,512]{1,0:T(8,128)(2,1)}, u32[]{:S(2)}) copy-start(bf16[64,512]{1,0:T(8,128)(2,1)} %constant.37.clone.pick) | copy-start | bytes 196612
  0.0 24.7 %copy-start = (s32[3,2048]{1,0:T(4,128)S(1)}, s32[3,2048]{1,0:T(4,128)}, u32[]{:S(2)}) copy-start(s32[3,2048]{1,0:T(4,128)} %waves.1) | copy-start | bytes 73732
  1.6 23.1 %all-to-all-start = ((bf16[32,2,8,128]{3,2,1,0:T(8,128)(2,1)}), bf16[32,2,8,128]{3,2,1,0:T(8,128)(2,1)S(1)}, u32[]{:S(2)}, u32[]{:S(2)}) async-start(bf16[32,2,8,128]{3,2,1,0:T(8,128)(2,1)} %order.1), calls=%async_computation | async-start | bytes 262144 | tf_op jit(solution)/shard_map/all_to_all | solution.py:259
  54.0 4.9 %collective-permute-start = (bf16[16,16,256]{2,1,0:T(8,128)(2,1)S(1)}, bf16[16,16,256]{2,1,0:T(8,128)(2,1)S(1)}, u32[]{:S(2)}, u32[]{:S(2)}) collective-permute-start(bf16[16,16,256]{2,1,0:T(8,128)(2,1)S(1)} %get-tuple-element.18), channel_id=1, source_target_pairs={{0,8},{8,0},{1,9},{9,1},{2,10},{10,2},{3,11},{11,3},{4,12},{12,4},... | collective-permute-start | bytes 393224 | tf_op jit(solution)/shard_map/ppermute | solution.py:315

commit v5 on v4

--- a/solution.py
+++ b/solution.py
@@ -158,23 +158,24 @@
     w = weight[...]
     for z in range(8):
         wt = w * total[:, 128 * z:128 * (z + 1)]
-        for t in range(8):
-            out[z * 8 + t] = jnp.concatenate(
-                [wt, total[:, 128 * t:128 * (t + 1)]], axis=0
+        for y in range(4):
+            out[z * 4 + y] = jnp.concatenate(
+                [wt, total[:, 128 * y:128 * (y + 1)], total[:, 128 * y + 512:128 * y + 640]], axis=0
             ).astype(jnp.bfloat16)
 
 
 def chi_kernel(recv, own, send, buf):
     upper = lax.axis_index("c") == 1
-    buf[...] = recv[...].astype(jnp.float32).reshape(1024, 128)
+    buf[...] = recv[...].astype(jnp.float32).reshape(768, 128)
 
     def rows(kind, h, j, c):
-        return buf[pl.ds(8 * kind + 4 * h + 2 * j + c, 64, stride=16), :]
+        return buf[pl.ds(8 * kind + 4 * h + 2 * j + c, 32, stride=24), :]
 
     right = jnp.concatenate(
         [
-            jnp.concatenate([rows(1, h, j, c) for c in range(2) for j in range(2)], axis=0)
+            jnp.concatenate([rows(1 + p, h, j, c) for c in range(2) for j in range(2)], axis=0)
             for h in range(2)
+            for p in range(2)
         ],
         axis=1,
     ).astype(jnp.bfloat16)
@@ -188,7 +189,7 @@
         ).astype(jnp.bfloat16)
         chi = lax.dot_general(left, right, dims, preferred_element_type=jnp.float32)
         chi = jnp.concatenate(
-            [chi[:128].reshape(16, 8, 256), chi[128:].reshape(16, 8, 256)], axis=1
+            [chi[:128].reshape(16, 8, 512), chi[128:].reshape(16, 8, 512)], axis=1
         )
         low, high = chi[:8], chi[8:]
         own[8 * h:8 * (h + 1)] = jnp.where(upper, high, low).astype(jnp.bfloat16)
@@ -200,12 +201,16 @@
 
 
 def final_kernel(recv, out):
-    for b in range(8):
-        acc = recv[b].astype(jnp.float32) + recv[8 + b].astype(jnp.float32)
+    for y in range(4):
+        acc = recv[y].astype(jnp.float32)
+        for s in range(1, 4):
+            acc = acc + recv[4 * s + y].astype(jnp.float32)
         for h in range(2):
-            lane = h * 1024 + b * 128
-            out[0, :, lane:lane + 128] = acc[:8, 128 * h:128 * (h + 1)]
-            out[1, :, lane:lane + 128] = acc[8:, 128 * h:128 * (h + 1)]
+            for p in range(2):
+                lane = h * 1024 + p * 512 + y * 128
+                part = acc[:, 256 * h + 128 * p:256 * h + 128 * (p + 1)]
+                out[0, :, lane:lane + 128] = part[:8]
+                out[1, :, lane:lane + 128] = part[8:]
 
 
 VM = pl.BlockSpec(memory_space=pltpu.VMEM)
@@ -303,17 +308,17 @@
         mib=8,
     )(vbuf, phase, cond, wave_vectors, ymat, zmat, pick)
     recv = lax.all_to_all(partial, BAND, split_axis=0, concat_axis=0, tiled=True)
-    packed = call(pack_kernel, "pack", ((64, 16, 128), BF16), [VM, VM])(weight, recv)
-    recv = lax.all_to_all(packed, ("z",) + BAND, split_axis=0, concat_axis=0, tiled=True)
+    packed = call(pack_kernel, "pack", ((32, 24, 128), BF16), [VM, VM])(weight, recv)
+    recv = lax.all_to_all(packed, ("z", "y"), split_axis=0, concat_axis=0, tiled=True)
     own, send = call(
         chi_kernel,
         "chi",
-        [((16, 16, 256), BF16)] * 2,
+        [((16, 16, 512), BF16)] * 2,
         [VM],
-        [pltpu.VMEM((1024, 128), F32)],
+        [pltpu.VMEM((768, 128), F32)],
     )(recv)
     other = lax.ppermute(send, "c", [(0, 1), (1, 0)])
-    merged = call(merge_kernel, "merge", ((16, 16, 256), BF16), [VM, VM])(own, other)
+    merged = call(merge_kernel, "merge", ((16, 16, 512), BF16), [VM, VM])(own, other)
     recv = lax.all_to_all(merged, ("xh",) + BAND, split_axis=0, concat_axis=0, tiled=True)
     return call(final_kernel, "final", ((2, 8, NG), F32), [VM])(recv)
 

time: 70 us -> 68.7 us (0.981)
  blocking collectives: 34.6 us -> 33 us
    all_to_all x1, blocking collectives: 15.1 us -> 13.3 us  [shards(): lax.all_to_all(packed, ('z', 'y'), split_axis=0, concat_axis=0, tiled=True)]
  transfers between devices with their start and end apart: 2 -> 2, of which waited for: 2 -> 2; matrix products, arithmetic and copies ran while one was open for 1% -> 1% of each run, Pallas kernels for 4% -> 5%
where the time goes in v5:
time: 68.7 us; the launch traced here: 68.4 us
  blocking collectives  33 us (48%)
  starting transfers between devices  16.5 us (24%)
  Pallas kernels  10.2 us (15%)
  waiting for transfers between devices  7.22 us (11%)
  between operations  0.71 us (1%)
    all_to_all x1, blocking collectives, shards(): lax.all_to_all(packed, ('z', 'y'), split_axis=0, concat_axis=0, tiled=True)  13.3 us
    all_to_all x1, starting transfers between devices, shards(): cond = lax.all_to_all(ordered, KA, split_axis=0, concat_axis=0, tiled=True)  12.6 us
    all_to_all x1, blocking collectives, shards(): lax.all_to_all(merged, ('xh',) + BAND, split_axis=0, concat_axis=0, tiled...  10.3 us
    all_to_all x1, blocking collectives, shards(): lax.all_to_all(partial, BAND, split_axis=0, concat_axis=0, tiled=True)  9.45 us
    all_to_all x1, waiting for transfers between devices, shards(): cond = lax.all_to_all(ordered, KA, split_axis=0, concat_axis=0, tiled=True)  6.06 us
    pallas_call x1, Pallas kernels, shards(): call(density_kernel, 'density', ((8, 8, 1024), BF16), [VM] * 7, [pltpu.VM...  4.3 us
    ppermute x1, starting transfers between devices, shards(): other = lax.ppermute(send, 'c', [(0, 1), (1, 0)])  3.96 us
    pallas_call x1, Pallas kernels, shards(): call(prep_kernel, 'prep', [((16, NG), F32), ((8, 128), F32), ((NOCC, GRID...  3.12 us
  transfers between devices with their start and end apart: 2, of which 2 were waited for; matrix products, arithmetic and copies ran while one was open for 1% of the time, Pallas kernels for 5%

profile of v5, /device:TPU:1, one launch (start us, length us, event | category | flops | bytes accessed | tf_op | source)
XLA Modules:
  0.0 68.4 jit_solution(8159913936324557412)
XLA Ops:
  0.0 0.0 copy-start.1
  0.0 0.0 copy-start
  0.0 1.6 %order.1 = bf16[32,2,8,128]{3,2,1,0:T(8,128)(2,1)} custom-call(s32[32]{0:T(128)} %shift.1, bf16[32,1,2,8,128]{4,3,2,1,0:T(8,128)(2,1)} %cond.1), custom_call_target="tpu_custom_call" | custom-call | tf_op jit(solution)/shard_map/order/pallas_call | solution.py:252
  1.6 12.6 %all-to-all-start = ((bf16[32,2,8,128]{3,2,1,0:T(8,128)(2,1)}), bf16[32,2,8,128]{3,2,1,0:T(8,128)(2,1)S(1)}, u32[]{:S(2)}, u32[]{:S(2)}) async-start(bf16[32,2,8,128]{3,2,1,0:T(8,128)(2,1)} %order.1), calls=%async_computation | async-start | bytes 262144 | tf_op jit(solution)/shard_map/all_to_all | solution.py:264
  14.9 0.7 pad_add_fusion.ids
  15.5 3.1 %prep.1 = (f32[16,2048]{1,0:T(8,128)S(1)}, f32[8,128]{1,0:T(8,128)S(1)}, bf16[16,64,8,128]{3,2,1,0:T(8,128)(2,1)S(1)}, bf16[512,512]{1,0:T(8,128)(2,1)S(1)}, bf16[1024,256]{1,0:T(8,128)(2,1)S(1)}) custom-call(s32[2]{0:T(128)} %pad_add_fusion.ids, s32[1,16]{1,0:T(1,128)} %sel_h.1, s32[32]{0:T(128)} %shift.1, f32[1,32]{1,0:T(1,128)} %vale_h.1, f32[32]{0:T(128)} %bitcast.3, ...), custom_call_target="tpu_custom_call" | custom-call | flops 67108864 | bytes 1048576 | tf_op jit(solution)/shard_map/prep/pallas_call | solution.py:265
  18.7 6.1 %all-to-all-done.cond = bf16[32,2,8,128]{3,2,1,0:T(8,128)(2,1)S(1)} async-done(((bf16[32,2,8,128]{3,2,1,0:T(8,128)(2,1)}), bf16[32,2,8,128]{3,2,1,0:T(8,128)(2,1)S(1)}, u32[]{:S(2)}, u32[]{:S(2)}) %all-to-all-start) | async-done | bytes 131104 | tf_op jit(solution)/shard_map/all_to_all | solution.py:264
  24.7 0.0 copy-done.1
  24.7 0.0 copy-done
  24.7 4.3 %density.1 = bf16[8,8,1024]{2,1,0:T(8,128)(2,1)S(1)} custom-call(bf16[16,64,8,128]{3,2,1,0:T(8,128)(2,1)S(1)} %get-tuple-element.13.vbuf, f32[16,2048]{1,0:T(8,128)S(1)} %get-tuple-element.14.phase, bf16[32,2,8,128]{3,2,1,0:T(8,128)(2,1)S(1)} %all-to-all-done.cond, s32[3,2048]{1,0:T(4,128)S(1)} %copy-done, bf16[512,512]{1,0:T(8,128)(2,1)S(1)} %get-tuple-element.15.ymat, ...), custom_call_target="tpu_custom_call" | custom-call | tf_op jit(solution)/shard_map/density/pallas_call | solution.py:296
  29.0 9.4 %all_to_all.20.recv = bf16[8,8,1024]{2,1,0:T(8,128)(2,1)S(1)} all-to-all(bf16[8,8,1024]{2,1,0:T(8,128)(2,1)S(1)} %density.1), channel_id=1, replica_groups=mesh['xh'=2,'z'=8,'c'=2,'xl'=2,'y'=4] {'xl','y'}, dimensions={0} | all-to-all | bytes 262144 | tf_op jit(solution)/shard_map/all_to_all | solution.py:310
  38.5 13.3 %all_to_all.21.recv = bf16[32,24,128]{2,1,0:T(8,128)(2,1)S(1)} all-to-all(bf16[32,24,128]{2,1,0:T(8,128)(2,1)S(1)} %pack.1), channel_id=1, replica_groups=mesh['xh'=2,'z'=8,'c'=2,'xl'=2,'y'=4] {'z','y'}, dimensions={0} | all-to-all | bytes 393216 | tf_op jit(solution)/shard_map/all_to_all | solution.py:312
  51.9 0.3 chi.1
  52.2 4.0 %collective-permute-start = (bf16[16,16,512]{2,1,0:T(8,128)(2,1)S(1)}, bf16[16,16,512]{2,1,0:T(8,128)(2,1)S(1)}, u32[]{:S(2)}, u32[]{:S(2)}) collective-permute-start(bf16[16,16,512]{2,1,0:T(8,128)(2,1)S(1)} %get-tuple-element.18), channel_id=1, source_target_pairs={{0,8},{8,0},{1,9},{9,1},{2,10},{10,2},{3,11},{11,3},{4,12},{12,4},... | collective-permute-start | bytes 786440 | tf_op jit(solution)/shard_map/ppermute | solution.py:320
  56.2 1.2 %collective-permute-done.other = bf16[16,16,512]{2,1,0:T(8,128)(2,1)S(1)} collective-permute-done((bf16[16,16,512]{2,1,0:T(8,128)(2,1)S(1)}, bf16[16,16,512]{2,1,0:T(8,128)(2,1)S(1)}, u32[]{:S(2)}, u32[]{:S(2)}) %collective-permute-start) | collective-permute-done | bytes 262176 | tf_op jit(solution)/shard_map/ppermute | solution.py:320
  57.3 0.1 merge.1
  57.4 10.3 %all_to_all.22.recv = bf16[16,16,512]{2,1,0:T(8,128)(2,1)S(1)} all-to-all(bf16[16,16,512]{2,1,0:T(8,128)(2,1)S(1)} %merge.1), channel_id=1, replica_groups=mesh['xh'=2,'z'=8,'c'=2,'xl'=2,'y'=4] {'xh','xl','y'}, dimensions={0} | all-to-all | bytes 524288 | tf_op jit(solution)/shard_map/all_to_all | solution.py:322
  67.7 0.7 %final.1 = f32[2,8,2048]{2,1,0:T(8,128)} custom-call(bf16[16,16,512]{2,1,0:T(8,128)(2,1)S(1)} %all_to_all.22.recv), custom_call_target="tpu_custom_call" | custom-call | tf_op jit(solution)/shard_map/final/pallas_call | solution.py:323
  (1 shorter events, 0.0 us)
Async XLA Ops:
  0.0 24.7 %copy-start.1 = (bf16[64,512]{1,0:T(8,128)(2,1)S(1)}, bf16[64,512]{1,0:T(8,128)(2,1)}, u32[]{:S(2)}) copy-start(bf16[64,512]{1,0:T(8,128)(2,1)} %constant.37.clone.pick) | copy-start | bytes 196612
  0.0 24.7 %copy-start = (s32[3,2048]{1,0:T(4,128)S(1)}, s32[3,2048]{1,0:T(4,128)}, u32[]{:S(2)}) copy-start(s32[3,2048]{1,0:T(4,128)} %waves.1) | copy-start | bytes 73732
  1.6 23.1 %all-to-all-start = ((bf16[32,2,8,128]{3,2,1,0:T(8,128)(2,1)}), bf16[32,2,8,128]{3,2,1,0:T(8,128)(2,1)S(1)}, u32[]{:S(2)}, u32[]{:S(2)}) async-start(bf16[32,2,8,128]{3,2,1,0:T(8,128)(2,1)} %order.1), calls=%async_computation | async-start | bytes 262144 | tf_op jit(solution)/shard_map/all_to_all | solution.py:264
  52.2 5.1 %collective-permute-start = (bf16[16,16,512]{2,1,0:T(8,128)(2,1)S(1)}, bf16[16,16,512]{2,1,0:T(8,128)(2,1)S(1)}, u32[]{:S(2)}, u32[]{:S(2)}) collective-permute-start(bf16[16,16,512]{2,1,0:T(8,128)(2,1)S(1)} %get-tuple-element.18), channel_id=1, source_target_pairs={{0,8},{8,0},{1,9},{9,1},{2,10},{10,2},{3,11},{11,3},{4,12},{12,4},... | collective-permute-start | bytes 786440 | tf_op jit(solution)/shard_map/ppermute | solution.py:320

commit v6 on v5

--- a/solution.py
+++ b/solution.py
@@ -114,8 +114,8 @@
             j = 2 * p + q
             v = vbuf[j].reshape(512, 128)
             pair = v * c1[...] + pltpu.roll(v, GRID, 1) * c2[...]
-            pbuf[p % 2, :, 128 * q:128 * (q + 1)] = pair
-        g = jnp.dot(ymat[...], pbuf[p % 2], preferred_element_type=jnp.float32)
+            pbuf[p, :, 128 * q:128 * (q + 1)] = pair
+        g = jnp.dot(ymat[...], pbuf[p], preferred_element_type=jnp.float32)
         g = g.reshape(2, HALF, SLAB, 256)
         g = jnp.concatenate([g[..., :128], g[..., 128:]], axis=2).astype(jnp.bfloat16)
         for w in range(2):
@@ -301,7 +301,7 @@
         [
             pltpu.VMEM((512, 128), BF16),
             pltpu.VMEM((512, 128), BF16),
-            pltpu.VMEM((2, 512, 256), BF16),
+            pltpu.VMEM((8, 512, 256), BF16),
             pltpu.VMEM((1024, 1024), BF16),
             pltpu.VMEM((256, 1024), BF16),
         ],

time: 68.7 us -> 68.6 us (level)
  no operation moved by 1% of the time
where the time goes in v6:
time: 68.6 us; the launch traced here: 68.3 us
  blocking collectives  33.1 us (48%)
  starting transfers between devices  16.5 us (24%)
  Pallas kernels  10.1 us (15%)
  waiting for transfers between devices  7.22 us (11%)
  between operations  0.71 us (1%)
    all_to_all x1, blocking collectives, shards(): lax.all_to_all(packed, ('z', 'y'), split_axis=0, concat_axis=0, tiled=True)  13.3 us
    all_to_all x1, starting transfers between devices, shards(): cond = lax.all_to_all(ordered, KA, split_axis=0, concat_axis=0, tiled=True)  12.6 us
    all_to_all x1, blocking collectives, shards(): lax.all_to_all(merged, ('xh',) + BAND, split_axis=0, concat_axis=0, tiled...  10.3 us
    all_to_all x1, blocking collectives, shards(): lax.all_to_all(partial, BAND, split_axis=0, concat_axis=0, tiled=True)  9.45 us
    all_to_all x1, waiting for transfers between devices, shards(): cond = lax.all_to_all(ordered, KA, split_axis=0, concat_axis=0, tiled=True)  6.06 us
    pallas_call x1, Pallas kernels, shards(): call(density_kernel, 'density', ((8, 8, 1024), BF16), [VM] * 7, [pltpu.VM...  4.21 us
    ppermute x1, starting transfers between devices, shards(): other = lax.ppermute(send, 'c', [(0, 1), (1, 0)])  3.94 us
    pallas_call x1, Pallas kernels, shards(): call(prep_kernel, 'prep', [((16, NG), F32), ((8, 128), F32), ((NOCC, GRID...  3.12 us
  transfers between devices with their start and end apart: 2, of which 2 were waited for; matrix products, arithmetic and copies ran while one was open for 1% of the time, Pallas kernels for 5%

profile of v6, /device:TPU:1, one launch (start us, length us, event | category | flops | bytes accessed | tf_op | source)
XLA Modules:
  0.0 68.3 jit_solution(8754094873693000662)
XLA Ops:
  0.0 0.0 copy-start.1
  0.0 0.0 copy-start
  0.0 1.6 %order.1 = bf16[32,2,8,128]{3,2,1,0:T(8,128)(2,1)} custom-call(s32[32]{0:T(128)} %shift.1, bf16[32,1,2,8,128]{4,3,2,1,0:T(8,128)(2,1)} %cond.1), custom_call_target="tpu_custom_call" | custom-call | tf_op jit(solution)/shard_map/order/pallas_call | solution.py:252
  1.6 12.6 %all-to-all-start = ((bf16[32,2,8,128]{3,2,1,0:T(8,128)(2,1)}), bf16[32,2,8,128]{3,2,1,0:T(8,128)(2,1)S(1)}, u32[]{:S(2)}, u32[]{:S(2)}) async-start(bf16[32,2,8,128]{3,2,1,0:T(8,128)(2,1)} %order.1), calls=%async_computation | async-start | bytes 262144 | tf_op jit(solution)/shard_map/all_to_all | solution.py:264
  14.9 0.7 pad_add_fusion.ids
  15.5 3.1 %prep.1 = (f32[16,2048]{1,0:T(8,128)S(1)}, f32[8,128]{1,0:T(8,128)S(1)}, bf16[16,64,8,128]{3,2,1,0:T(8,128)(2,1)S(1)}, bf16[512,512]{1,0:T(8,128)(2,1)S(1)}, bf16[1024,256]{1,0:T(8,128)(2,1)S(1)}) custom-call(s32[2]{0:T(128)} %pad_add_fusion.ids, s32[1,16]{1,0:T(1,128)} %sel_h.1, s32[32]{0:T(128)} %shift.1, f32[1,32]{1,0:T(1,128)} %vale_h.1, f32[32]{0:T(128)} %bitcast.3, ...), custom_call_target="tpu_custom_call" | custom-call | flops 67108864 | bytes 1048576 | tf_op jit(solution)/shard_map/prep/pallas_call | solution.py:265
  18.7 6.1 %all-to-all-done.cond = bf16[32,2,8,128]{3,2,1,0:T(8,128)(2,1)S(1)} async-done(((bf16[32,2,8,128]{3,2,1,0:T(8,128)(2,1)}), bf16[32,2,8,128]{3,2,1,0:T(8,128)(2,1)S(1)}, u32[]{:S(2)}, u32[]{:S(2)}) %all-to-all-start) | async-done | bytes 131104 | tf_op jit(solution)/shard_map/all_to_all | solution.py:264
  24.7 0.0 copy-done.1
  24.7 0.0 copy-done
  24.7 4.2 %density.1 = bf16[8,8,1024]{2,1,0:T(8,128)(2,1)S(1)} custom-call(bf16[16,64,8,128]{3,2,1,0:T(8,128)(2,1)S(1)} %get-tuple-element.13.vbuf, f32[16,2048]{1,0:T(8,128)S(1)} %get-tuple-element.14.phase, bf16[32,2,8,128]{3,2,1,0:T(8,128)(2,1)S(1)} %all-to-all-done.cond, s32[3,2048]{1,0:T(4,128)S(1)} %copy-done, bf16[512,512]{1,0:T(8,128)(2,1)S(1)} %get-tuple-element.15.ymat, ...), custom_call_target="tpu_custom_call" | custom-call | tf_op jit(solution)/shard_map/density/pallas_call | solution.py:296
  29.0 9.5 %all_to_all.20.recv = bf16[8,8,1024]{2,1,0:T(8,128)(2,1)S(1)} all-to-all(bf16[8,8,1024]{2,1,0:T(8,128)(2,1)S(1)} %density.1), channel_id=1, replica_groups=mesh['xh'=2,'z'=8,'c'=2,'xl'=2,'y'=4] {'xl','y'}, dimensions={0} | all-to-all | bytes 262144 | tf_op jit(solution)/shard_map/all_to_all | solution.py:310
  38.4 13.3 %all_to_all.21.recv = bf16[32,24,128]{2,1,0:T(8,128)(2,1)S(1)} all-to-all(bf16[32,24,128]{2,1,0:T(8,128)(2,1)S(1)} %pack.1), channel_id=1, replica_groups=mesh['xh'=2,'z'=8,'c'=2,'xl'=2,'y'=4] {'z','y'}, dimensions={0} | all-to-all | bytes 393216 | tf_op jit(solution)/shard_map/all_to_all | solution.py:312
  51.8 0.3 chi.1
  52.1 3.9 %collective-permute-start = (bf16[16,16,512]{2,1,0:T(8,128)(2,1)S(1)}, bf16[16,16,512]{2,1,0:T(8,128)(2,1)S(1)}, u32[]{:S(2)}, u32[]{:S(2)}) collective-permute-start(bf16[16,16,512]{2,1,0:T(8,128)(2,1)S(1)} %get-tuple-element.18), channel_id=1, source_target_pairs={{0,8},{8,0},{1,9},{9,1},{2,10},{10,2},{3,11},{11,3},{4,12},{12,4},... | collective-permute-start | bytes 786440 | tf_op jit(solution)/shard_map/ppermute | solution.py:320
  56.1 1.2 %collective-permute-done.other = bf16[16,16,512]{2,1,0:T(8,128)(2,1)S(1)} collective-permute-done((bf16[16,16,512]{2,1,0:T(8,128)(2,1)S(1)}, bf16[16,16,512]{2,1,0:T(8,128)(2,1)S(1)}, u32[]{:S(2)}, u32[]{:S(2)}) %collective-permute-start) | collective-permute-done | bytes 262176 | tf_op jit(solution)/shard_map/ppermute | solution.py:320
  57.2 0.1 merge.1
  57.3 10.3 %all_to_all.22.recv = bf16[16,16,512]{2,1,0:T(8,128)(2,1)S(1)} all-to-all(bf16[16,16,512]{2,1,0:T(8,128)(2,1)S(1)} %merge.1), channel_id=1, replica_groups=mesh['xh'=2,'z'=8,'c'=2,'xl'=2,'y'=4] {'xh','xl','y'}, dimensions={0} | all-to-all | bytes 524288 | tf_op jit(solution)/shard_map/all_to_all | solution.py:322
  67.6 0.7 %final.1 = f32[2,8,2048]{2,1,0:T(8,128)} custom-call(bf16[16,16,512]{2,1,0:T(8,128)(2,1)S(1)} %all_to_all.22.recv), custom_call_target="tpu_custom_call" | custom-call | tf_op jit(solution)/shard_map/final/pallas_call | solution.py:323
  (1 shorter events, 0.0 us)
Async XLA Ops:
  0.0 24.7 %copy-start.1 = (bf16[64,512]{1,0:T(8,128)(2,1)S(1)}, bf16[64,512]{1,0:T(8,128)(2,1)}, u32[]{:S(2)}) copy-start(bf16[64,512]{1,0:T(8,128)(2,1)} %constant.37.clone.pick) | copy-start | bytes 196612
  0.0 24.7 %copy-start = (s32[3,2048]{1,0:T(4,128)S(1)}, s32[3,2048]{1,0:T(4,128)}, u32[]{:S(2)}) copy-start(s32[3,2048]{1,0:T(4,128)} %waves.1) | copy-start | bytes 73732
  1.6 23.1 %all-to-all-start = ((bf16[32,2,8,128]{3,2,1,0:T(8,128)(2,1)}), bf16[32,2,8,128]{3,2,1,0:T(8,128)(2,1)S(1)}, u32[]{:S(2)}, u32[]{:S(2)}) async-start(bf16[32,2,8,128]{3,2,1,0:T(8,128)(2,1)} %order.1), calls=%async_computation | async-start | bytes 262144 | tf_op jit(solution)/shard_map/all_to_all | solution.py:264
  52.1 5.1 %collective-permute-start = (bf16[16,16,512]{2,1,0:T(8,128)(2,1)S(1)}, bf16[16,16,512]{2,1,0:T(8,128)(2,1)S(1)}, u32[]{:S(2)}, u32[]{:S(2)}) collective-permute-start(bf16[16,16,512]{2,1,0:T(8,128)(2,1)S(1)} %get-tuple-element.18), channel_id=1, source_target_pairs={{0,8},{8,0},{1,9},{9,1},{2,10},{10,2},{3,11},{11,3},{4,12},{12,4},... | collective-permute-start | bytes 786440 | tf_op jit(solution)/shard_map/ppermute | solution.py:320
